TPU v7x, 32 devices: a whole 2x2x4 slice. The times are simulated.
32 devices in a mesh: grp: 2 (over y), seq: 8 (over z, x), head: 2 (over core).
Axes of the slice: x: 2, y: 2, z: 4, core: 2. Of those that a mesh axis runs over, the one named last changes fastest.
Arguments:
- queries: bfloat16 [8192, 4096], P(('grp', 'seq'), 'head'), parts along dimension 0, may hold values from -64 to 64
- keys: bfloat16 [8192, 512], P(('grp', 'seq'), 'head'), parts along dimension 0, may hold values from -6 to 6
- values: bfloat16 [8192, 512], P(('grp', 'seq'), 'head'), parts along dimension 0, may hold values from -6 to 6
- levels: int32 [8192], P(('grp', 'seq')), parts along dimension 0, may hold values from 0 to 3
- members: int32 [16, 4], P(('grp', 'seq')), parts along dimension 0, may hold values from -1 to 31, as said below
Outputs:
- attended: bfloat16 [8192, 4096], P(('grp', 'seq'), 'head'), parts along dimension 0
There are 2 independent parts, one for each index of `grp`. A program takes and returns all parts, laid end to end along the dimension named above; each array names one. Nothing has to cross between parts.
Inputs may be any that keep to these rules, and one draw needn't show every extreme that they name: `members`: slot j of row d is -1 or one of the 4 blocks of group d + o_j; a slot whose group lies outside 0 to 7 is -1; some group lists a block in every slot.
All inputs are finite; a program needn't handle non-finite values.
Results may differ from a plain program's by a relative error of at most 0.005.
Values may be sent and summed in bfloat16 or wider, within the bound.
No kernel may reach another device: no remote copies, remote signals or barrier semaphores. Data moves between devices by JAX's collectives and lax.ppermute only.
A program may use at most 128 MiB of HBM per device.

v0:
```python
import jax
import jax.numpy as jnp
from jax import lax
from jax.sharding import PartitionSpec as P

HD = 128
QHEADS = 32
KVHEADS = 4
BLOCK = 128
RADIUS = 2


def shifted(array, axis, by):
    size = lax.axis_size(axis)
    pairs = [(i, i + by) for i in range(size) if 0 <= i + by < size]
    return lax.ppermute(array, axis, pairs)


def local(queries, keys, values, levels, members):
    tok_rows = queries.shape[0]
    kv_heads = keys.shape[1] // HD
    group_size = QHEADS // KVHEADS
    scaling = HD ** (-0.5)
    blocks_dev = tok_rows // BLOCK
    query_heads = queries.reshape(tok_rows, kv_heads, group_size, HD)
    query_level = levels.astype(jnp.float32)
    position = lax.axis_index("seq")
    offsets = list(range(-RADIUS, 0)) + list(range(1, RADIUS + 1))

    def attend(state, key_rows, value_rows, key_level, active):
        running, total, accum = state
        key_heads = key_rows.reshape(-1, kv_heads, HD)
        value_heads = value_rows.reshape(-1, kv_heads, HD)
        scores = (
            jnp.einsum("tkgd,skd->tkgs", query_heads, key_heads, preferred_element_type=jnp.float32)
            * scaling
        )
        visible = jnp.logical_and(active, key_level[None, :] <= query_level[:, None])
        scores = jnp.where(visible[:, None, None, :], scores, -1e30)
        newest = jnp.maximum(running, jnp.max(scores, axis=-1))
        factor = jnp.exp(running - newest)
        weights = jnp.exp(scores - newest[..., None])
        total = total * factor + jnp.sum(weights, axis=-1)
        update = jnp.einsum(
            "tkgs,skd->tkgd",
            weights.astype(jnp.bfloat16),
            value_heads,
            preferred_element_type=jnp.float32,
        )
        accum = accum * factor[..., None] + update
        return (newest, total, accum)

    state = (
        jnp.full((tok_rows, kv_heads, group_size), -1e30, jnp.float32),
        jnp.zeros((tok_rows, kv_heads, group_size), jnp.float32),
        jnp.zeros((tok_rows, kv_heads, group_size, HD), jnp.float32),
    )
    state = attend(state, keys, values, query_level, True)
    level_wire = levels.astype(jnp.bfloat16)
    for column, offset in enumerate(offsets):
        far_keys, far_values, far_levels = shifted((keys, values, level_wire), "seq", -offset)
        entry = members[0, column]
        within = jnp.clip(entry - (position + offset) * blocks_dev, 0, blocks_dev - 1) * BLOCK
        picked_keys = lax.dynamic_slice_in_dim(far_keys, within, BLOCK, 0)
        picked_values = lax.dynamic_slice_in_dim(far_values, within, BLOCK, 0)
        picked_levels = lax.dynamic_slice_in_dim(far_levels, within, BLOCK, 0)
        state = attend(
            state, picked_keys, picked_values, picked_levels.astype(jnp.float32), entry >= 0
        )
    running, total, accum = state
    mixed = accum / total[..., None]
    return mixed.reshape(tok_rows, kv_heads * group_size * HD).astype(jnp.bfloat16)


def solution(mesh):
    placed = (
        P(("grp", "seq"), "head"),
        P(("grp", "seq"), "head"),
        P(("grp", "seq"), "head"),
        P(("grp", "seq")),
        P(("grp", "seq"), None),
    )
    return jax.shard_map(
        local, mesh=mesh, in_specs=placed, out_specs=P(("grp", "seq"), "head"), check_vma=False
    )
```

profile of v0, /device:TPU:10, one launch (start us, length us, event | category | flops | bytes accessed | tf_op | source)
XLA Modules:
  0.0 125.4 jit_solution(15809584164581785991)
XLA Ops:
  0.0 0.8 fusion.71
  0.8 2.3 %collective-permute-start.9 = (bf16[512]{0:T(512)(128)(2,1)S(1)}, bf16[512]{0:T(512)(128)(2,1)S(1)}, u32[]{:S(2)}, u32[]{:S(2)}) collective-permute-start(bf16[512]{0:T(512)(128)(2,1)S(1)} %get-tuple-element.20), channel_id=1, source_target_pairs={{4,0},{6,2},{8,4},{10,6},{12,8},{14,10},{5,1},{7,3},{9,5},{11,7},{... | collective-permute-start | bytes 3080 | tf_op jit(solution)/shard_map/ppermute | solution.py:16
  3.1 2.0 %collective-permute-start.6 = (bf16[512]{0:T(512)(128)(2,1)S(1)}, bf16[512]{0:T(512)(128)(2,1)S(1)}, u32[]{:S(2)}, u32[]{:S(2)}) collective-permute-start(bf16[512]{0:T(512)(128)(2,1)S(1)} %get-tuple-element.20), channel_id=1, source_target_pairs={{2,0},{4,2},{6,4},{8,6},{10,8},{12,10},{14,12},{3,1},{5,3},{7,5},{... | collective-permute-start | bytes 3080 | tf_op jit(solution)/shard_map/ppermute | solution.py:16
  5.1 4.7 %collective-permute-start.3 = (bf16[512]{0:T(512)(128)(2,1)S(1)}, bf16[512]{0:T(512)(128)(2,1)S(1)}, u32[]{:S(2)}, u32[]{:S(2)}) collective-permute-start(bf16[512]{0:T(512)(128)(2,1)S(1)} %get-tuple-element.20), channel_id=1, source_target_pairs={{0,2},{2,4},{4,6},{6,8},{8,10},{10,12},{12,14},{1,3},{3,5},{5,7},{... | collective-permute-start | bytes 3080 | tf_op jit(solution)/shard_map/ppermute | solution.py:16
  9.9 3.5 %collective-permute-start = (bf16[512]{0:T(512)(128)(2,1)S(1)}, bf16[512]{0:T(512)(128)(2,1)S(1)}, u32[]{:S(2)}, u32[]{:S(2)}) collective-permute-start(bf16[512]{0:T(512)(128)(2,1)S(1)} %get-tuple-element.20), channel_id=1, source_target_pairs={{0,4},{2,6},{4,8},{6,10},{8,12},{10,14},{1,5},{3,7},{5,9},{7,11},{... | collective-permute-start | bytes 3080 | tf_op jit(solution)/shard_map/ppermute | solution.py:16
  13.4 1.1 copy.27
  14.5 2.4 %collective-permute-start.10 = (bf16[512,256]{0,1:T(8,128)(2,1)S(1)}, bf16[512,256]{0,1:T(8,128)(2,1)}, u32[]{:S(2)}, u32[]{:S(2)}) collective-permute-start(bf16[512,256]{0,1:T(8,128)(2,1)S(1)} %copy.27), channel_id=1, source_target_pairs={{4,0},{6,2},{8,4},{10,6},{12,8},{14,10},{5,1},{7,3},{9,5},{11,7},{... | collective-permute-start | bytes 786440 | tf_op jit(solution)/shard_map/ppermute | solution.py:16
  16.8 1.5 %fusion.72 = (s32[1,1]{1,0:T(1,128)}, s32[1,1]{1,0:T(1,128)}, s32[1,1]{1,0:T(1,128)}, s32[1,1]{1,0:T(1,128)}) fusion(s32[1,4]{1,0:T(1,128)} %param.9), kind=kLoop, calls=%fused_computation.105 | loop fusion | bytes 32 | tf_op jit(solution)/shard_map/slice | solution.py:62
  20.1 1.0 reshape.251
  21.1 2.2 %copy.74 = bf16[64,8,16,128]{3,2,1,0:T(8,128)(2,1)S(1)} copy(bf16[64,8,16,128]{3,1,2,0:T(8,128)(2,1)} %bitcast.143) | data formatting | bytes 4194304
  23.3 0.2 broadcast_compare_fusion
  23.5 0.0 copy-start.6
  23.6 7.5 %fusion.2 = (f32[512,2,8]{0,2,1:T(8,128)S(1)}, f32[2,512,512,8]{2,1,3,0:T(8,128)}) fusion(pred[512,512]{0,1:T(8,128)(4,1)S(1)} %broadcast_compare_fusion, bf16[512,2,8,128]{3,2,1,0:T(8,128)(2,1)S(1)} %bitcast.138, bf16[512,2,128,1]{2,1,0,3:T(2,128)(2,1)S(1)} %bitcast.145), kind=kOutput, calls=%fused_computation.4 | convolution fusion | flops 1086316544 | bytes 19431424 | tf_op jit(solution)/shard_map/tkgd,skd->tkgs/dot_general | solution.py:35
  34.2 0.1 copy.65
  34.3 0.0 collective-permute-done.9
  34.3 1.9 %collective-permute-start.7 = (bf16[512,256]{0,1:T(8,128)(2,1)S(1)}, bf16[512,256]{0,1:T(8,128)(2,1)S(1)}, u32[]{:S(2)}, u32[]{:S(2)}) collective-permute-start(bf16[512,256]{0,1:T(8,128)(2,1)S(1)} %copy.27), channel_id=1, source_target_pairs={{2,0},{4,2},{6,4},{8,6},{10,8},{12,10},{14,12},{3,1},{5,3},{7,5},{... | collective-permute-start | bytes 786440 | tf_op jit(solution)/shard_map/ppermute | solution.py:16
  36.3 0.1 dynamic-slice_convert_fusion
  36.3 0.0 collective-permute-done.6
  36.3 4.8 %collective-permute-start.4 = (bf16[512,256]{0,1:T(8,128)(2,1)S(1)}, bf16[512,256]{0,1:T(8,128)(2,1)S(1)}, u32[]{:S(2)}, u32[]{:S(2)}) collective-permute-start(bf16[512,256]{0,1:T(8,128)(2,1)S(1)} %copy.27), channel_id=1, source_target_pairs={{0,2},{2,4},{4,6},{6,8},{8,10},{10,12},{12,14},{1,3},{3,5},{5,7},{... | collective-permute-start | bytes 786440 | tf_op jit(solution)/shard_map/ppermute | solution.py:16
  41.2 0.1 dynamic-slice_convert_fusion.1
  41.2 0.0 collective-permute-done.3
  41.3 3.5 %collective-permute-start.1 = (bf16[512,256]{0,1:T(8,128)(2,1)S(1)}, bf16[512,256]{0,1:T(8,128)(2,1)S(1)}, u32[]{:S(2)}, u32[]{:S(2)}) collective-permute-start(bf16[512,256]{0,1:T(8,128)(2,1)S(1)} %copy.27), channel_id=1, source_target_pairs={{0,4},{2,6},{4,8},{6,10},{8,12},{10,14},{1,5},{3,7},{5,9},{7,11},{... | collective-permute-start | bytes 786440 | tf_op jit(solution)/shard_map/ppermute | solution.py:16
  44.7 0.1 dynamic-slice_convert_fusion.2
  44.8 0.0 collective-permute-done
  44.8 1.9 %collective-permute-start.2 = (bf16[512,256]{1,0:T(8,128)(2,1)S(1)}, bf16[512,256]{1,0:T(8,128)(2,1)}, u32[]{:S(2)}, u32[]{:S(2)}) collective-permute-start(bf16[512,256]{1,0:T(8,128)(2,1)S(1)} %copy-done.6), channel_id=1, source_target_pairs={{0,4},{2,6},{4,8},{6,10},{8,12},{10,14},{1,5},{3,7},{5,9},{7,11},{... | collective-permute-start | bytes 786440 | tf_op jit(solution)/shard_map/ppermute | solution.py:16
  46.7 0.1 dynamic-slice_convert_fusion.3
  46.8 0.2 compare_and_fusion.3
  47.1 0.0 collective-permute-done.10
  47.1 2.4 %collective-permute-start.5 = (bf16[512,256]{1,0:T(8,128)(2,1)S(1)}, bf16[512,256]{1,0:T(8,128)(2,1)}, u32[]{:S(2)}, u32[]{:S(2)}) collective-permute-start(bf16[512,256]{1,0:T(8,128)(2,1)S(1)} %copy-done.6), channel_id=1, source_target_pairs={{0,2},{2,4},{4,6},{6,8},{8,10},{10,12},{12,14},{1,3},{3,5},{5,7},{... | collective-permute-start | bytes 786440 | tf_op jit(solution)/shard_map/ppermute | solution.py:16
  49.4 0.9 constant_dynamic-slice_fusion.1
  50.3 3.6 %fusion.23 = (f32[512,2,8]{0,2,1:T(8,128)S(1)}, f32[2,128,512,8]{2,1,3,0:T(8,128)}) fusion(pred[512,128]{0,1:T(8,128)(4,1)S(1)} %get-tuple-element.19, bf16[128,2,128,1]{0,2,3,1:T(8,128)(2,1)S(1)} %bitcast.150, bf16[512,2,8,128]{3,2,1,0:T(8,128)(2,1)S(1)} %bitcast.139), kind=kOutput, calls=%fused_computation.37 | convolution fusion | flops 271572992 | bytes 6455296 | tf_op jit(solution)/shard_map/tkgd,skd->tkgs/dot_general | solution.py:35
  53.9 0.0 collective-permute-done.7
  53.9 3.5 %collective-permute-start.8 = (bf16[512,256]{1,0:T(8,128)(2,1)S(1)}, bf16[512,256]{1,0:T(8,128)(2,1)}, u32[]{:S(2)}, u32[]{:S(2)}) collective-permute-start(bf16[512,256]{1,0:T(8,128)(2,1)S(1)} %copy-done.6), channel_id=1, source_target_pairs={{2,0},{4,2},{6,4},{8,6},{10,8},{12,10},{14,12},{3,1},{5,3},{7,5},{... | collective-permute-start | bytes 786440 | tf_op jit(solution)/shard_map/ppermute | solution.py:16
  57.4 3.6 %fusion.22 = (f32[512,2,8]{0,2,1:T(8,128)S(1)}, f32[2,128,512,8]{2,1,3,0:T(8,128)}) fusion(pred[512,128]{0,1:T(8,128)(4,1)S(1)} %get-tuple-element.18, bf16[128,2,128,1]{0,2,3,1:T(8,128)(2,1)S(1)} %bitcast.151, bf16[512,2,8,128]{3,2,1,0:T(8,128)(2,1)S(1)} %bitcast.140), kind=kOutput, calls=%fused_computation.36 | convolution fusion | flops 271572992 | bytes 6455296 | tf_op jit(solution)/shard_map/tkgd,skd->tkgs/dot_general | solution.py:35
  61.0 0.0 collective-permute-done.4
  61.0 5.5 %collective-permute-start.11 = (bf16[512,256]{1,0:T(8,128)(2,1)S(1)}, bf16[512,256]{1,0:T(8,128)(2,1)}, u32[]{:S(2)}, u32[]{:S(2)}) collective-permute-start(bf16[512,256]{1,0:T(8,128)(2,1)S(1)} %copy-done.6), channel_id=1, source_target_pairs={{4,0},{6,2},{8,4},{10,6},{12,8},{14,10},{5,1},{7,3},{9,5},{11,7},{... | collective-permute-start | bytes 786440 | tf_op jit(solution)/shard_map/ppermute | solution.py:16
  66.5 3.6 %fusion.21 = (f32[512,2,8]{0,2,1:T(8,128)S(1)}, f32[2,128,512,8]{2,1,3,0:T(8,128)}) fusion(pred[512,128]{0,1:T(8,128)(4,1)S(1)} %get-tuple-element.17, bf16[128,2,128,1]{0,2,3,1:T(8,128)(2,1)S(1)} %bitcast.152, bf16[512,2,8,128]{3,2,1,0:T(8,128)(2,1)S(1)} %bitcast.141), kind=kOutput, calls=%fused_computation.35 | convolution fusion | flops 271572992 | bytes 6455296 | tf_op jit(solution)/shard_map/tkgd,skd->tkgs/dot_general | solution.py:35
  70.1 0.0 collective-permute-done.1
  70.1 3.7 %fusion.20 = (f32[512,2,8]{0,2,1:T(8,128)S(1)}, f32[2,128,512,8]{2,1,3,0:T(8,128)}) fusion(pred[512,128]{0,1:T(8,128)(4,1)S(1)} %get-tuple-element.16, bf16[128,2,128,1]{0,2,3,1:T(8,128)(2,1)S(1)} %bitcast.149, bf16[512,2,8,128]{3,2,1,0:T(8,128)(2,1)S(1)} %bitcast.142), kind=kOutput, calls=%fused_computation.34 | convolution fusion | flops 271572992 | bytes 6455296 | tf_op jit(solution)/shard_map/tkgd,skd->tkgs/dot_general | solution.py:35
  73.9 9.2 %fusion = f32[512,2,8]{0,2,1:T(8,128)S(1)} fusion(f32[2,512,512,8]{2,1,3,0:T(8,128)} %get-tuple-element.35, f32[512,2,8]{0,2,1:T(8,128)S(1)} %get-tuple-element.15, pred[512,512]{0,1:T(8,128)(4,1)S(1)} %broadcast_compare_fusion), kind=kLoop, calls=%fused_computation.2 | loop fusion | flops 16769024 | bytes 17104896 | tf_op jit(solution)/shard_map/reduce_sum | solution.py:43
  83.0 12.2 %fusion.3 = f32[2,512,8,128]{1,3,2,0:T(8,128)} fusion(bf16[512,2,128,1]{0,2,3,1:T(8,128)(2,1)S(1)} %bitcast.153, f32[2,512,512,8]{2,1,3,0:T(8,128)} %get-tuple-element.35, f32[512,2,8]{0,2,1:T(8,128)S(1)} %get-tuple-element.15, pred[512,512]{0,1:T(8,128)(4,1)S(1)} %broadcast_compare_fusion), kind=kOutput, calls=%fused_computation.5 | convolution fusion | flops 1090519040 | bytes 21528576 | tf_op jit(solution)/shard_map/tkgs,skd->tkgd/dot_general | solution.py:44
  95.2 0.0 collective-permute-done.2
  95.2 0.8 constant_dynamic-slice_fusion.6
  96.0 0.1 copy.30
  96.2 0.0 collective-permute-done.5
  96.2 0.9 constant_dynamic-slice_fusion.4
  97.0 0.1 copy.35
  97.1 0.0 collective-permute-done.8
  97.2 0.9 constant_dynamic-slice_fusion.2
  98.0 0.1 copy.40
  98.1 5.8 %fusion.29 = f32[2,128,512,8]{2,1,3,0:T(8,128)} fusion(bf16[128,2,128,1]{0,2,3,1:T(8,128)(2,1)S(1)} %bitcast.148, f32[2,128,512,8]{2,1,3,0:T(8,128)} %get-tuple-element.33, f32[512,2,8]{0,2,1:T(8,128)S(1)} %get-tuple-element.13, pred[512,128]{0,1:T(8,128)(4,1)S(1)} %get-tuple-element.16), kind=kOutput, calls=%fused_computation.40 | convolution fusion | flops 272629760 | bytes 8552448 | tf_op jit(solution)/shard_map/tkgs,skd->tkgd/dot_general | solution.py:44
  104.0 0.0 copy-done.1
  104.0 2.1 %fusion.12 = (f32[512,2,8]{0,2,1:T(8,128)S(1)}, f32[512,2,8]{0,2,1:T(8,128)S(1)}) fusion(f32[2,128,512,8]{2,1,3,0:T(8,128)S(1)} %copy-done.2, f32[512,2,8]{0,2,1:T(8,128)S(1)} %get-tuple-element.13, pred[512,128]{0,1:T(8,128)(4,1)S(1)} %get-tuple-element.16, f32[512,2,8]{0,2,1:T(8,128)S(1)} %get-tuple-element.12, f32[2,128,512,8]{2,1,3,0:T(8,128)S(1)} %copy-done.1, ...), kind=kLoop, calls=%fused_computation.26 | loop fusion | flops 8372224 | bytes 8650752 | tf_op jit(solution)/shard_map/reduce_sum | solution.py:43
  106.1 3.4 %fusion.27 = f32[2,128,512,8]{2,1,3,0:T(8,128)} fusion(bf16[128,2,128,1]{0,2,3,1:T(8,128)(2,1)S(1)} %bitcast.147, f32[2,128,512,8]{2,1,3,0:T(8,128)S(1)} %copy-done.1, f32[512,2,8]{0,2,1:T(8,128)S(1)} %get-tuple-element.12, pred[512,128]{0,1:T(8,128)(4,1)S(1)} %get-tuple-element.17), kind=kOutput, calls=%fused_computation.39 | convolution fusion | flops 272629760 | bytes 8552448 | tf_op jit(solution)/shard_map/tkgs,skd->tkgd/dot_general | solution.py:44
  109.5 0.0 collective-permute-done.11
  109.5 0.8 constant_dynamic-slice_fusion
  110.3 0.1 copy.45
  110.4 3.7 %fusion.25 = f32[2,128,512,8]{2,1,3,0:T(8,128)S(1)} fusion(bf16[128,2,128,1]{0,2,3,1:T(8,128)(2,1)S(1)} %bitcast.146, f32[2,128,512,8]{2,1,3,0:T(8,128)} %get-tuple-element.29, f32[512,2,8]{0,2,1:T(8,128)S(1)} %get-tuple-element.11, pred[512,128]{0,1:T(8,128)(4,1)S(1)} %get-tuple-element.18), kind=kOutput, calls=%fused_computation.38 | convolution fusion | flops 272629760 | bytes 8552448 | tf_op jit(solution)/shard_map/tkgs,skd->tkgd/dot_general | solution.py:44
  114.2 1.0 copy-done.3
  115.2 2.1 %fusion.16 = (f32[512,2,8]{0,2,1:T(8,128)S(1)}, f32[512,2,8]{0,2,1:T(8,128)S(1)}) fusion(f32[2,128,512,8]{2,1,3,0:T(8,128)S(1)} %copy-done, f32[512,2,8]{0,2,1:T(8,128)S(1)} %get-tuple-element.11, pred[512,128]{0,1:T(8,128)(4,1)S(1)} %get-tuple-element.18, f32[512,2,8]{0,2,1:T(8,128)S(1)} %get-tuple-element.10, f32[2,128,512,8]{2,1,3,0:T(8,128)S(1)} %copy-done.3, ...), kind=kLoop, calls=%fused_computation.30 | loop fusion | flops 8372224 | bytes 8650752 | tf_op jit(solution)/shard_map/reduce_sum | solution.py:43
  117.3 0.1 copy-done.4
  117.3 1.3 %copy-done.5 = f32[2,128,512,8]{2,1,3,0:T(8,128)S(1)} copy-done((f32[2,128,512,8]{2,1,3,0:T(8,128)S(1)}, f32[2,128,512,8]{2,1,3,0:T(8,128)}, u32[]{:S(2)}) %copy-start.5) | copy-done | bytes 4194328
  118.6 4.4 %fusion.7 = bf16[512,2,8,128]{0,3,2,1:T(8,128)(2,1)S(1)} fusion(f32[2,128,512,8]{2,1,3,0:T(8,128)S(1)} %fusion.25, f32[2,128,512,8]{2,1,3,0:T(8,128)S(1)} %copy-done.5, f32[2,128,512,8]{2,1,3,0:T(8,128)S(1)} %copy-done.4, f32[2,512,8,128]{1,3,2,0:T(8,128)} %fusion.3, bf16[128,2,128,1]{0,2,3,1:T(8,128)(2,1)S(1)} %bitcast.154, ...), kind=kOutput, calls=%fused_computation.9 | convolution fusion | flops 284164096 | bytes 23429120 | tf_op jit(solution)/shard_map/tkgs,skd->tkgd/dot_general | solution.py:44
  123.1 2.4 %copy.47 = bf16[512,2048]{1,0:T(8,128)(2,1)} copy(bf16[512,2048]{0,1:T(8,128)(2,1)S(1)} %bitcast.144) | data formatting | bytes 4194304 | tf_op jit(solution)/shard_map/convert_element_type | solution.py:72
  (14 shorter events, 0.1 us)
Async XLA Ops:
  0.8 33.6 %collective-permute-start.9 = (bf16[512]{0:T(512)(128)(2,1)S(1)}, bf16[512]{0:T(512)(128)(2,1)S(1)}, u32[]{:S(2)}, u32[]{:S(2)}) collective-permute-start(bf16[512]{0:T(512)(128)(2,1)S(1)} %get-tuple-element.20), channel_id=1, source_target_pairs={{4,0},{6,2},{8,4},{10,6},{12,8},{14,10},{5,1},{7,3},{9,5},{11,7},{... | collective-permute-start | bytes 3080 | tf_op jit(solution)/shard_map/ppermute | solution.py:16
  3.1 33.2 %collective-permute-start.6 = (bf16[512]{0:T(512)(128)(2,1)S(1)}, bf16[512]{0:T(512)(128)(2,1)S(1)}, u32[]{:S(2)}, u32[]{:S(2)}) collective-permute-start(bf16[512]{0:T(512)(128)(2,1)S(1)} %get-tuple-element.20), channel_id=1, source_target_pairs={{2,0},{4,2},{6,4},{8,6},{10,8},{12,10},{14,12},{3,1},{5,3},{7,5},{... | collective-permute-start | bytes 3080 | tf_op jit(solution)/shard_map/ppermute | solution.py:16
  5.1 36.1 %collective-permute-start.3 = (bf16[512]{0:T(512)(128)(2,1)S(1)}, bf16[512]{0:T(512)(128)(2,1)S(1)}, u32[]{:S(2)}, u32[]{:S(2)}) collective-permute-start(bf16[512]{0:T(512)(128)(2,1)S(1)} %get-tuple-element.20), channel_id=1, source_target_pairs={{0,2},{2,4},{4,6},{6,8},{8,10},{10,12},{12,14},{1,3},{3,5},{5,7},{... | collective-permute-start | bytes 3080 | tf_op jit(solution)/shard_map/ppermute | solution.py:16
  9.9 35.0 %collective-permute-start = (bf16[512]{0:T(512)(128)(2,1)S(1)}, bf16[512]{0:T(512)(128)(2,1)S(1)}, u32[]{:S(2)}, u32[]{:S(2)}) collective-permute-start(bf16[512]{0:T(512)(128)(2,1)S(1)} %get-tuple-element.20), channel_id=1, source_target_pairs={{0,4},{2,6},{4,8},{6,10},{8,12},{10,14},{1,5},{3,7},{5,9},{7,11},{... | collective-permute-start | bytes 3080 | tf_op jit(solution)/shard_map/ppermute | solution.py:16
  14.5 32.6 %collective-permute-start.10 = (bf16[512,256]{0,1:T(8,128)(2,1)S(1)}, bf16[512,256]{0,1:T(8,128)(2,1)}, u32[]{:S(2)}, u32[]{:S(2)}) collective-permute-start(bf16[512,256]{0,1:T(8,128)(2,1)S(1)} %copy.27), channel_id=1, source_target_pairs={{4,0},{6,2},{8,4},{10,6},{12,8},{14,10},{5,1},{7,3},{9,5},{11,7},{... | collective-permute-start | bytes 786440 | tf_op jit(solution)/shard_map/ppermute | solution.py:16
  23.5 10.6 %copy-start.6 = (bf16[512,256]{1,0:T(8,128)(2,1)S(1)}, bf16[512,256]{1,0:T(8,128)(2,1)}, u32[]{:S(2)}) copy-start(bf16[512,256]{1,0:T(8,128)(2,1)} %param.7) | copy-start | bytes 786436
  34.3 19.5 %collective-permute-start.7 = (bf16[512,256]{0,1:T(8,128)(2,1)S(1)}, bf16[512,256]{0,1:T(8,128)(2,1)S(1)}, u32[]{:S(2)}, u32[]{:S(2)}) collective-permute-start(bf16[512,256]{0,1:T(8,128)(2,1)S(1)} %copy.27), channel_id=1, source_target_pairs={{2,0},{4,2},{6,4},{8,6},{10,8},{12,10},{14,12},{3,1},{5,3},{7,5},{... | collective-permute-start | bytes 786440 | tf_op jit(solution)/shard_map/ppermute | solution.py:16
  36.3 24.7 %collective-permute-start.4 = (bf16[512,256]{0,1:T(8,128)(2,1)S(1)}, bf16[512,256]{0,1:T(8,128)(2,1)S(1)}, u32[]{:S(2)}, u32[]{:S(2)}) collective-permute-start(bf16[512,256]{0,1:T(8,128)(2,1)S(1)} %copy.27), channel_id=1, source_target_pairs={{0,2},{2,4},{4,6},{6,8},{8,10},{10,12},{12,14},{1,3},{3,5},{5,7},{... | collective-permute-start | bytes 786440 | tf_op jit(solution)/shard_map/ppermute | solution.py:16
  41.3 28.9 %collective-permute-start.1 = (bf16[512,256]{0,1:T(8,128)(2,1)S(1)}, bf16[512,256]{0,1:T(8,128)(2,1)S(1)}, u32[]{:S(2)}, u32[]{:S(2)}) collective-permute-start(bf16[512,256]{0,1:T(8,128)(2,1)S(1)} %copy.27), channel_id=1, source_target_pairs={{0,4},{2,6},{4,8},{6,10},{8,12},{10,14},{1,5},{3,7},{5,9},{7,11},{... | collective-permute-start | bytes 786440 | tf_op jit(solution)/shard_map/ppermute | solution.py:16
  44.8 50.4 %collective-permute-start.2 = (bf16[512,256]{1,0:T(8,128)(2,1)S(1)}, bf16[512,256]{1,0:T(8,128)(2,1)}, u32[]{:S(2)}, u32[]{:S(2)}) collective-permute-start(bf16[512,256]{1,0:T(8,128)(2,1)S(1)} %copy-done.6), channel_id=1, source_target_pairs={{0,4},{2,6},{4,8},{6,10},{8,12},{10,14},{1,5},{3,7},{5,9},{7,11},{... | collective-permute-start | bytes 786440 | tf_op jit(solution)/shard_map/ppermute | solution.py:16
  47.1 49.1 %collective-permute-start.5 = (bf16[512,256]{1,0:T(8,128)(2,1)S(1)}, bf16[512,256]{1,0:T(8,128)(2,1)}, u32[]{:S(2)}, u32[]{:S(2)}) collective-permute-start(bf16[512,256]{1,0:T(8,128)(2,1)S(1)} %copy-done.6), channel_id=1, source_target_pairs={{0,2},{2,4},{4,6},{6,8},{8,10},{10,12},{12,14},{1,3},{3,5},{5,7},{... | collective-permute-start | bytes 786440 | tf_op jit(solution)/shard_map/ppermute | solution.py:16
  53.9 43.3 %collective-permute-start.8 = (bf16[512,256]{1,0:T(8,128)(2,1)S(1)}, bf16[512,256]{1,0:T(8,128)(2,1)}, u32[]{:S(2)}, u32[]{:S(2)}) collective-permute-start(bf16[512,256]{1,0:T(8,128)(2,1)S(1)} %copy-done.6), channel_id=1, source_target_pairs={{2,0},{4,2},{6,4},{8,6},{10,8},{12,10},{14,12},{3,1},{5,3},{7,5},{... | collective-permute-start | bytes 786440 | tf_op jit(solution)/shard_map/ppermute | solution.py:16
  61.0 48.4 %collective-permute-start.11 = (bf16[512,256]{1,0:T(8,128)(2,1)S(1)}, bf16[512,256]{1,0:T(8,128)(2,1)}, u32[]{:S(2)}, u32[]{:S(2)}) collective-permute-start(bf16[512,256]{1,0:T(8,128)(2,1)S(1)} %copy-done.6), channel_id=1, source_target_pairs={{4,0},{6,2},{8,4},{10,6},{12,8},{14,10},{5,1},{7,3},{9,5},{11,7},{... | collective-permute-start | bytes 786440 | tf_op jit(solution)/shard_map/ppermute | solution.py:16
  98.1 5.9 %copy-start.1 = (f32[2,128,512,8]{2,1,3,0:T(8,128)S(1)}, f32[2,128,512,8]{2,1,3,0:T(8,128)}, u32[]{:S(2)}) copy-start(f32[2,128,512,8]{2,1,3,0:T(8,128)} %get-tuple-element.31) | copy-start | bytes 12582916
  98.1 5.9 %copy-start.2 = (f32[2,128,512,8]{2,1,3,0:T(8,128)S(1)}, f32[2,128,512,8]{2,1,3,0:T(8,128)}, u32[]{:S(2)}) copy-start(f32[2,128,512,8]{2,1,3,0:T(8,128)} %get-tuple-element.33) | copy-start | bytes 12582916
  110.4 3.7 %copy-start = (f32[2,128,512,8]{2,1,3,0:T(8,128)S(1)}, f32[2,128,512,8]{2,1,3,0:T(8,128)}, u32[]{:S(2)}) copy-start(f32[2,128,512,8]{2,1,3,0:T(8,128)} %get-tuple-element.29) | copy-start | bytes 12582916
  110.4 4.7 %copy-start.3 = (f32[2,128,512,8]{2,1,3,0:T(8,128)S(1)}, f32[2,128,512,8]{2,1,3,0:T(8,128)}, u32[]{:S(2)}) copy-start(f32[2,128,512,8]{2,1,3,0:T(8,128)} %get-tuple-element.27) | copy-start | bytes 12582916
  115.2 2.2 %copy-start.4 = (f32[2,128,512,8]{2,1,3,0:T(8,128)S(1)}, f32[2,128,512,8]{2,1,3,0:T(8,128)}, u32[]{:S(2)}) copy-start(f32[2,128,512,8]{2,1,3,0:T(8,128)} %fusion.29) | copy-start | bytes 12582916
  115.2 3.5 %copy-start.5 = (f32[2,128,512,8]{2,1,3,0:T(8,128)S(1)}, f32[2,128,512,8]{2,1,3,0:T(8,128)}, u32[]{:S(2)}) copy-start(f32[2,128,512,8]{2,1,3,0:T(8,128)} %fusion.27) | copy-start | bytes 12582916
where the time goes:
time: 126 us; the launch traced here: 125 us
  matrix products  51.5 us (41%)
  starting transfers between devices  38.4 us (30%)
  local copies, waits for them, and re-layouts  15.4 us (12%)
  other arithmetic  14.9 us (12%)
  between operations  5.25 us (4%)
    ppermute x12, starting transfers between devices, shifted(): return lax.ppermute(array, axis, pairs)  38.4 us
    dot_general x5, matrix products, attend(): jnp.einsum('tkgs,skd->tkgd', weights.astype(jnp.bfloat16), value_heads, p...  29.5 us
    dot_general x5, matrix products, attend(): jnp.einsum('tkgd,skd->tkgs', query_heads, key_heads, preferred_element_ty...  22 us
    reduce_sum x3, other arithmetic, attend(): total = total * factor + jnp.sum(weights, axis=-1)  13.3 us
    unnamed x16, local copies, waits for them, and re-layouts  5.66 us
    dynamic_slice x8, local copies, waits for them, and re-layouts, local(): picked_values = lax.dynamic_slice_in_dim(far_values, within, BLOCK, 0)  3.83 us
  transfers between devices with their start and end apart: 12, of which 0 were waited for; matrix products, arithmetic and copies ran while one was open for 52% of the time, Pallas kernels for 0%

commit v1 on v0

v1 whole, which is shorter than its diff:
```python
import functools

import jax
import jax.numpy as jnp
from jax import lax
from jax.experimental import pallas as pl
from jax.experimental.pallas import tpu as pltpu
from jax.sharding import PartitionSpec as P

HD = 128
BLOCK = 128
RADIUS = 2
GROUP = 8
ROWS = 128
PAD = 16
SCALE = HD ** (-0.5) * 1.4426950408889634
HIDDEN = -1e30
NT = (((1,), (1,)), ((), ()))
NN = (((1,), (0,)), ((), ()))


def column_of(row):
    return jnp.broadcast_to(row, (HD, row.shape[1])).T


def bias_of(query_level, key_level):
    wide = jnp.concatenate([query_level] * (key_level.shape[1] // HD), axis=1)
    return jnp.where(key_level <= wide, 0.0, HIDDEN)


def own_kernel(kv_heads, q_ref, k_ref, v_ref, level_ref, o_ref, lse_ref, bias_ref, vx_ref):
    tok = q_ref.shape[0]
    level = level_ref[...].astype(jnp.float32)
    bias_ref[...] = bias_of(column_of(level), level)
    lane = lax.broadcasted_iota(jnp.int32, (ROWS, HD), 1)
    vx_ref[:, HD:] = jnp.ones((tok, HD), jnp.bfloat16)
    lse_ref[...] = jnp.zeros_like(lse_ref)

    def step(g, carry):
        base = pl.multiple_of(g * (GROUP * HD), GROUP * HD)
        cols = pl.ds(pl.multiple_of(g * HD, HD), HD)
        vx_ref[:, :HD] = v_ref[:, cols]
        for r in range(0, tok, ROWS):
            rows = pl.ds(r, ROWS)
            lse = lse_ref[rows, :]
            for h in range(GROUP):
                head = pl.ds(base + h * HD, HD)
                s = lax.dot_general(q_ref[rows, head], k_ref[:, cols], NT, preferred_element_type=jnp.float32)
                s = s * SCALE + bias_ref[rows, :]
                top = jnp.max(s, axis=1, keepdims=True)
                p = jnp.exp2(s - top).astype(jnp.bfloat16)
                o = lax.dot_general(p, vx_ref[...], NN, preferred_element_type=jnp.float32)
                total = o[:, HD:]
                o_ref[rows, head] = o[:, :HD] / total
                lse = jnp.where(lane == g * GROUP + h, top + jnp.log2(total), lse)
            lse_ref[rows, :] = lse
        return carry

    lax.fori_loop(0, kv_heads, step, 0)


def far_kernel(
    kv_heads, pick_ref, q_ref, level_ref, o_ref, lse_ref, lo_ref, near_ref, diag_ref, hi_ref, out_ref,
    bias_ref, kx_ref, vx_ref, kl_ref,
):
    tok = q_ref.shape[0]
    g = pl.program_id(0)
    far = kx_ref.shape[0]

    @pl.when(g == 0)
    def _():
        for slot, (ref, index) in enumerate(((lo_ref, 0), (near_ref, 1), (diag_ref, 2), (hi_ref, 3))):
            if ref is diag_ref:
                level = ref[BLOCK : BLOCK + 1, :BLOCK]
            else:
                first = pl.multiple_of(pick_ref[index] * BLOCK, BLOCK)
                level = ref[tok : tok + 1, pl.ds(first, BLOCK)]
            level = level.astype(jnp.float32)
            kl_ref[0:1, slot * BLOCK : (slot + 1) * BLOCK] = jnp.where(pick_ref[4 + index] > 0, level, 1e9)
        query_level = column_of(level_ref[...].astype(jnp.float32))
        bias_ref[...] = bias_of(query_level, kl_ref[0:1, :])
        vx_ref[:, HD:] = jnp.ones((far, HD), jnp.bfloat16)

    cols = pl.ds(pl.multiple_of(g * HD, HD), HD)
    vcols = pl.ds(pl.multiple_of((g + kv_heads) * HD, HD), HD)
    for slot, (ref, index) in enumerate(((lo_ref, 0), (near_ref, 1), (diag_ref, 2), (hi_ref, 3))):
        if ref is diag_ref:
            first = pl.ds(0, BLOCK)
        else:
            first = pl.ds(pl.multiple_of(pick_ref[index] * BLOCK, BLOCK), BLOCK)
        kx_ref[slot * BLOCK : (slot + 1) * BLOCK, :] = ref[first, cols]
        vx_ref[slot * BLOCK : (slot + 1) * BLOCK, :HD] = ref[first, vcols]
    lane = lax.broadcasted_iota(jnp.int32, (ROWS, HD), 1)
    for r in range(0, tok, ROWS):
        rows = pl.ds(r, ROWS)
        lse_all = lse_ref[rows, :]
        for h in range(GROUP):
            head = pl.ds(pl.multiple_of(g * (GROUP * HD), GROUP * HD) + h * HD, HD)
            own = jnp.max(jnp.where(lane == g * GROUP + h, lse_all, HIDDEN), axis=1, keepdims=True)
            s = lax.dot_general(q_ref[rows, head], kx_ref[...], NT, preferred_element_type=jnp.float32)
            s = s * SCALE + bias_ref[rows, :]
            top = jnp.maximum(jnp.max(s, axis=1, keepdims=True), own)
            p = jnp.exp2(s - top).astype(jnp.bfloat16)
            o = lax.dot_general(p, vx_ref[...], NN, preferred_element_type=jnp.float32)
            share = jnp.exp2(own - top)
            mixed = (o[:, :HD] + share * o_ref[rows, head]) / (o[:, HD:] + share)
            out_ref[rows, h * HD : (h + 1) * HD] = mixed.astype(jnp.bfloat16)


def pairs_of(size, kind):
    if kind == "near":
        edges = [(i, i + 1) for i in range(0, size - 1, 2)]
        return [p for a, b in edges for p in ((a, b), (b, a))]
    if kind == "diag":
        edges = [(i, i + 1) for i in range(1, size - 1, 2)]
        return [p for a, b in edges for p in ((a, b), (b, a))]
    return [(i, i + kind) for i in range(size) if 0 <= i + kind < size]


def local(queries, keys, values, levels, members):
    tok = queries.shape[0]
    kv_heads = keys.shape[1] // HD
    heads = queries.shape[1] // HD
    size = lax.axis_size("seq")
    position = lax.axis_index("seq")
    blocks = tok // BLOCK
    odd = lax.rem(position, 2)
    send = lambda array, kind: lax.ppermute(array, "seq", pairs_of(size, kind))

    width = 2 * keys.shape[1]
    level_row = jnp.pad(levels.astype(jnp.bfloat16)[None, :], ((0, PAD - 1), (0, width - tok)))
    load = jnp.concatenate([jnp.concatenate([keys, values], axis=1), level_row], axis=0)
    from_hi = send(load, -2)
    from_lo = send(load, 2)
    from_near = send(load, "near")

    asked = send(members, "diag")[0]
    asked = jnp.where(odd == 1, asked[1], asked[2])
    first = jnp.clip(asked - position * blocks, 0, blocks - 1) * BLOCK
    piece = lax.dynamic_slice_in_dim(load, first, BLOCK, 0)
    piece_level = jnp.pad(
        lax.dynamic_slice_in_dim(level_row, first, BLOCK, 1), ((0, 0), (0, width - BLOCK))
    )
    from_diag = send(jnp.concatenate([piece, piece_level], axis=0), "diag")

    level_line = levels[None, :]
    vmem = pl.BlockSpec(memory_space=pltpu.VMEM)
    part, lse = pl.pallas_call(
        functools.partial(own_kernel, kv_heads),
        in_specs=[vmem] * 4,
        out_specs=[vmem] * 2,
        out_shape=[
            jax.ShapeDtypeStruct((tok, heads * HD), jnp.float32),
            jax.ShapeDtypeStruct((tok, HD), jnp.float32),
        ],
        scratch_shapes=[pltpu.VMEM((tok, tok), jnp.float32), pltpu.VMEM((tok, 2 * HD), jnp.bfloat16)],
        compiler_params=pltpu.CompilerParams(vmem_limit_bytes=24 << 20),
        cost_estimate=pl.CostEstimate(
            flops=4 * tok * tok * heads * HD, transcendentals=tok * tok * heads, bytes_accessed=8 << 20
        ),
    )(queries, keys, values, level_line)

    row = members[0]
    near_slot = jnp.where(odd == 1, 1, 2)
    order = jnp.stack([row[0], jnp.where(odd == 1, row[1], row[2]), jnp.where(odd == 1, row[2], row[1]), row[3]])
    owner = position + jnp.stack([-2, 1 - 2 * odd, 2 * odd - 1, 2])
    pick = jnp.concatenate(
        [jnp.clip(order - owner * blocks, 0, blocks - 1), (order >= 0).astype(jnp.int32)]
    ).astype(jnp.int32)
    far = 2 * RADIUS * BLOCK
    full = lambda array: pl.BlockSpec(array.shape, lambda g, pick: (0, 0))
    return pl.pallas_call(
        functools.partial(far_kernel, kv_heads),
        grid_spec=pltpu.PrefetchScalarGridSpec(
            num_scalar_prefetch=1,
            grid=(kv_heads,),
            in_specs=[vmem] * 8,
            out_specs=pl.BlockSpec((tok, GROUP * HD), lambda g, pick: (0, g)),
            scratch_shapes=[
                pltpu.VMEM((tok, far), jnp.float32),
                pltpu.VMEM((far, HD), jnp.bfloat16),
                pltpu.VMEM((far, 2 * HD), jnp.bfloat16),
                pltpu.VMEM((8, far), jnp.float32),
            ],
        ),
        out_shape=jax.ShapeDtypeStruct((tok, heads * HD), jnp.bfloat16),
        compiler_params=pltpu.CompilerParams(vmem_limit_bytes=24 << 20),
        cost_estimate=pl.CostEstimate(
            flops=4 * tok * far * heads * HD, transcendentals=tok * far * heads, bytes_accessed=8 << 20
        ),
    )(pick, queries, level_line, part, lse, from_lo, from_near, from_diag, from_hi)


def solution(mesh):
    placed = (
        P(("grp", "seq"), "head"),
        P(("grp", "seq"), "head"),
        P(("grp", "seq"), "head"),
        P(("grp", "seq")),
        P(("grp", "seq"), None),
    )
    return jax.shard_map(
        local, mesh=mesh, in_specs=placed, out_specs=P(("grp", "seq"), "head"), check_vma=False
    )
```

time: 126 us -> 43.2 us (0.34)
  matrix products: 51.5 us -> 0 us
  starting transfers between devices: 38.4 us -> 16.1 us
  Pallas kernels: 0 us -> 14.8 us
  local copies, waits for them, and re-layouts: 15.4 us -> 2.86 us
  other arithmetic: 14.9 us -> 3.18 us
  waiting for transfers between devices: 0.03 us -> 2.26 us
  between operations: 5.25 us -> 3.76 us
    dot_general x10 -> x0, matrix products: 51.5 us -> none  [the longest x5 29.5 us: attend(): jnp.einsum('tkgs,skd->tkgd', weights.astype(jnp.bfloat16), value_heads, p...]
    ppermute x12 -> x5, starting transfers between devices: 38.4 us -> 16.1 us  [local(): send = lambda array, kind: lax.ppermute(array, 'seq', pairs_of(size, kind))]
    pallas_call x0 -> x2, Pallas kernels: none -> 14.8 us  [the longest x1 8.65 us: local(): pl.pallas_call(functools.partial(far_kernel, kv_heads), grid_spec=pltpu.P...]
    reduce_sum x3 -> x0, other arithmetic: 13.3 us -> none  [attend(): total = total * factor + jnp.sum(weights, axis=-1)]
    dynamic_slice x12 -> x2, local copies, waits for them, and re-layouts: 4.73 us -> 0.03 us  [the longest x1 0.02 us: local(): piece = lax.dynamic_slice_in_dim(load, first, BLOCK, 0)]
    unnamed x16 -> x10, local copies, waits for them, and re-layouts: 5.66 us -> 1.6 us
    convert_element_type x1 -> x0, local copies, waits for them, and re-layouts: 2.38 us -> none  [local(): mixed.reshape(tok_rows, kv_heads * group_size * HD).astype(jnp.bfloat16)]
    ppermute x12 -> x5, waiting for transfers between devices: 0.03 us -> 2.26 us  [local(): send = lambda array, kind: lax.ppermute(array, 'seq', pairs_of(size, kind))]
  transfers between devices with their start and end apart: 12 -> 5, of which waited for: 0 -> 1; matrix products, arithmetic and copies ran while one was open for 52% -> 6% of each run, Pallas kernels for 0% -> 14%
where the time goes in v1:
time: 43.2 us; the launch traced here: 42.9 us
  starting transfers between devices  16.1 us (37%)
  Pallas kernels  14.8 us (34%)
  between operations  3.76 us (9%)
  other arithmetic  3.18 us (7%)
  local copies, waits for them, and re-layouts  2.86 us (7%)
  waiting for transfers between devices  2.26 us (5%)
    ppermute x5, starting transfers between devices, local(): send = lambda array, kind: lax.ppermute(array, 'seq', pairs_of(size, kind))  16.1 us
    pallas_call x1, Pallas kernels, local(): pl.pallas_call(functools.partial(far_kernel, kv_heads), grid_spec=pltpu.P...  8.65 us
    pallas_call x1, Pallas kernels, local(): pl.pallas_call(functools.partial(own_kernel, kv_heads), in_specs=[vmem] *...  6.11 us
    ppermute x5, waiting for transfers between devices, local(): send = lambda array, kind: lax.ppermute(array, 'seq', pairs_of(size, kind))  2.26 us
    unnamed x10, local copies, waits for them, and re-layouts  1.6 us
    min x1, other arithmetic, local(): jnp.clip(order - owner * blocks, 0, blocks - 1)  1.27 us
    concatenate x1, other arithmetic, local(): jnp.concatenate([jnp.concatenate([keys, values], axis=1), level_row], axi...  1.06 us
  transfers between devices with their start and end apart: 5, of which 1 were waited for; matrix products, arithmetic and copies ran while one was open for 6% of the time, Pallas kernels for 14%

profile of v1, /device:TPU:10, one launch (start us, length us, event | category | flops | bytes accessed | tf_op | source)
XLA Modules:
  0.0 42.9 jit_solution(8820733689176185400)
XLA Ops:
  0.0 0.0 copy-start.3
  0.0 0.0 copy-start.2
  0.0 0.0 copy-start.1
  0.0 0.0 copy-start.4
  0.0 0.8 %convert_element_type.11 = bf16[512]{0:T(512)(128)(2,1)S(1)} convert(s32[512]{0:T(512)} %param.8) | non-fusion elementwise | flops 512 | bytes 3072 | tf_op jit(solution)/shard_map/convert_element_type | solution.py:131
  0.8 1.1 %pad_maximum_fusion = bf16[528,512]{1,0:T(8,128)(2,1)S(1)} fusion(bf16[16,512]{1,0:T(8,128)(2,1)S(1)} %pad.8, bf16[512,256]{1,0:T(8,128)(2,1)} %v_ref.1, bf16[512,256]{1,0:T(8,128)(2,1)} %k_ref.1), kind=kLoop, calls=%fused_computation | loop fusion | flops 1622016 | bytes 1081344 | tf_op jit(solution)/shard_map/concatenate | solution.py:132
  1.9 2.4 %collective-permute-start.4 = (bf16[528,512]{1,0:T(8,128)(2,1)S(1)}, bf16[528,512]{1,0:T(8,128)(2,1)S(1)}, u32[]{:S(2)}, u32[]{:S(2)}) collective-permute-start(bf16[528,512]{1,0:T(8,128)(2,1)S(1)} %pad_maximum_fusion), channel_id=1, source_target_pairs={{4,0},{6,2},{8,4},{10,6},{12,8},{14,10},{5,1},{7,3},{9,5},{11,7},{... | collective-permute-start | bytes 1622024 | tf_op jit(solution)/shard_map/ppermute | solution.py:128
  4.2 0.2 collective-permute-start.1
  4.4 3.9 %collective-permute-start = (bf16[528,512]{1,0:T(8,128)(2,1)S(1)}, bf16[528,512]{1,0:T(8,128)(2,1)S(1)}, u32[]{:S(2)}, u32[]{:S(2)}) collective-permute-start(bf16[528,512]{1,0:T(8,128)(2,1)S(1)} %pad_maximum_fusion), channel_id=1, source_target_pairs={{0,4},{2,6},{4,8},{6,10},{8,12},{10,14},{1,5},{3,7},{5,9},{7,11},{... | collective-permute-start | bytes 1622024 | tf_op jit(solution)/shard_map/ppermute | solution.py:128
  8.3 0.0 copy-done.4
  8.3 4.4 %collective-permute-start.2 = (s32[1,4]{1,0:T(1,128)S(1)}, s32[1,4]{1,0:T(1,128)S(1)}, u32[]{:S(2)}, u32[]{:S(2)}) collective-permute-start(s32[1,4]{1,0:T(1,128)S(1)} %copy-done.4), channel_id=1, source_target_pairs={{2,4},{4,2},{6,8},{8,6},{10,12},{12,10},{3,5},{5,3},{7,9},{9,7},{1... | collective-permute-start | bytes 56 | tf_op jit(solution)/shard_map/ppermute | solution.py:128
  12.8 0.6 %fusion.6 = (s32[1,1]{1,0:T(1,128)}, s32[1,1]{1,0:T(1,128)}, s32[1,1]{1,0:T(1,128)}, s32[1,1]{1,0:T(1,128)}) fusion(s32[1,4]{1,0:T(1,128)S(1)} %copy-done.4), kind=kLoop, calls=%fused_computation.14 | loop fusion | bytes 32 | tf_op jit(solution)/shard_map/slice | solution.py:165
  15.8 1.3 %fusion.4 = (s32[4]{0:T(128)S(1)}, s32[4]{0:T(128)S(1)}) fusion(s32[1]{0:T(128)} %constant.13.clone.1, s32[1]{0:T(128)} %bitcast.7, s32[1]{0:T(128)} %bitcast.6, s32[1]{0:T(128)} %constant.10.clone.1, s32[]{:T(128)S(6)} %axis_index.15, s32[1]{0:T(128)} %bitcast.5, s32[1]{0:T(128)} %bitcast.4, s32[1]{0:T(128)} %bitcast.3, s32[1]{0:T(128)} %bitcast), kind=kLoop, calls=%fused_computation.12 | loop fusion | flops 40 | bytes 68 | tf_op jit(solution)/shard_map/jit(clip)/min | solution.py:168
  17.1 2.2 %collective-permute-done.2 = s32[1,4]{1,0:T(1,128)S(1)} collective-permute-done((s32[1,4]{1,0:T(1,128)S(1)}, s32[1,4]{1,0:T(1,128)S(1)}, u32[]{:S(2)}, u32[]{:S(2)}) %collective-permute-start.2) | collective-permute-done | bytes 48 | tf_op jit(solution)/shard_map/ppermute | solution.py:128
  19.3 0.6 %fusion.5 = (s32[1,1]{1,0:T(1,128)}, s32[1,1]{1,0:T(1,128)}) fusion(s32[1,4]{1,0:T(1,128)S(1)} %collective-permute-done.2), kind=kLoop, calls=%fused_computation.13 | loop fusion | bytes 16 | tf_op jit(solution)/shard_map/slice | solution.py:138
  21.2 5.2 %collective-permute-start.3 = (bf16[144,512]{1,0:T(8,128)(2,1)S(1)}, bf16[144,512]{1,0:T(8,128)(2,1)S(1)}, u32[]{:S(2)}, u32[]{:S(2)}) collective-permute-start(bf16[144,512]{1,0:T(8,128)(2,1)S(1)} %fusion.1), channel_id=1, source_target_pairs={{2,4},{4,2},{6,8},{8,6},{10,12},{12,10},{3,5},{5,3},{7,9},{9,7},{1... | collective-permute-start | bytes 442376 | tf_op jit(solution)/shard_map/ppermute | solution.py:128
  26.4 0.0 copy-done.3
  26.4 0.0 copy-done.2
  26.4 0.0 copy-done.1
  26.4 0.0 copy-start
  26.5 1.6 %copy-done = bf16[512,2048]{1,0:T(8,128)(2,1)S(1)} copy-done((bf16[512,2048]{1,0:T(8,128)(2,1)S(1)}, bf16[512,2048]{1,0:T(8,128)(2,1)}, u32[]{:S(2)}) %copy-start) | copy-done | bytes 2097176
  28.0 6.1 %shard_map.55 = (f32[512,2048]{1,0:T(8,128)S(1)}, f32[512,128]{1,0:T(8,128)S(1)}) custom-call(bf16[512,2048]{1,0:T(8,128)(2,1)S(1)} %copy-done, bf16[512,256]{1,0:T(8,128)(2,1)S(1)} %copy-done.1, bf16[512,256]{1,0:T(8,128)(2,1)S(1)} %copy-done.2, s32[1,512]{1,0:T(1,128)S(1)} %bitcast.11), custom_call_target="tpu_custom_call" | custom-call | flops 2147483648 | bytes 8388608 | tf_op jit(solution)/shard_map/pallas_call | solution.py:148
  34.2 0.1 pad_add_fusion.1.pick_ref
  34.2 0.0 collective-permute-done.3.diag_ref
  34.2 0.0 collective-permute-done.4.hi_ref
  34.2 0.0 collective-permute-done.1.near_ref
  34.2 0.0 collective-permute-done.lo_ref
  34.3 8.7 %shard_map.56 = bf16[512,2048]{1,0:T(8,128)(2,1)} custom-call(s32[8]{0:T(128)S(1)} %pad_add_fusion.1.pick_ref, bf16[512,2048]{1,0:T(8,128)(2,1)S(1)} %copy-done, s32[1,512]{1,0:T(1,128)S(1)} %bitcast.12, f32[512,2048]{1,0:T(8,128)S(1)} %get-tuple-element.7.o_ref, f32[512,128]{1,0:T(8,128)S(1)} %get-tuple-element.8.lse_ref, ...), custom_call_target="tpu_custom_call" | custom-call | flops 2147483648 | bytes 8388608 | tf_op jit(solution)/shard_map/pallas_call | solution.py:172
  (6 shorter events, 0.1 us)
Async XLA Ops:
  0.0 26.4 %copy-start.3 = (s32[512]{0:T(512)S(1)}, s32[512]{0:T(512)}, u32[]{:S(2)}) copy-start(s32[512]{0:T(512)} %param.8) | copy-start | bytes 6148
  0.0 26.4 %copy-start.2 = (bf16[512,256]{1,0:T(8,128)(2,1)S(1)}, bf16[512,256]{1,0:T(8,128)(2,1)}, u32[]{:S(2)}) copy-start(bf16[512,256]{1,0:T(8,128)(2,1)} %v_ref.1) | copy-start | bytes 786436
  0.0 26.4 %copy-start.1 = (bf16[512,256]{1,0:T(8,128)(2,1)S(1)}, bf16[512,256]{1,0:T(8,128)(2,1)}, u32[]{:S(2)}) copy-start(bf16[512,256]{1,0:T(8,128)(2,1)} %k_ref.1) | copy-start | bytes 786436
  0.0 8.3 %copy-start.4 = (s32[1,4]{1,0:T(1,128)S(1)}, s32[1,4]{1,0:T(1,128)}, u32[]{:S(2)}) copy-start(s32[1,4]{1,0:T(1,128)} %param.9) | copy-start | bytes 52
  1.9 32.4 %collective-permute-start.4 = (bf16[528,512]{1,0:T(8,128)(2,1)S(1)}, bf16[528,512]{1,0:T(8,128)(2,1)S(1)}, u32[]{:S(2)}, u32[]{:S(2)}) collective-permute-start(bf16[528,512]{1,0:T(8,128)(2,1)S(1)} %pad_maximum_fusion), channel_id=1, source_target_pairs={{4,0},{6,2},{8,4},{10,6},{12,8},{14,10},{5,1},{7,3},{9,5},{11,7},{... | collective-permute-start | bytes 1622024 | tf_op jit(solution)/shard_map/ppermute | solution.py:128
  4.2 30.0 %collective-permute-start.1 = (bf16[528,512]{1,0:T(8,128)(2,1)S(1)}, bf16[528,512]{1,0:T(8,128)(2,1)S(1)}, u32[]{:S(2)}, u32[]{:S(2)}) collective-permute-start(bf16[528,512]{1,0:T(8,128)(2,1)S(1)} %pad_maximum_fusion), channel_id=1, source_target_pairs={{0,2},{2,0},{4,6},{6,4},{8,10},{10,8},{12,14},{14,12},{1,3},{3,1},... | collective-permute-start | bytes 1622024 | tf_op jit(solution)/shard_map/ppermute | solution.py:128
  4.4 29.9 %collective-permute-start = (bf16[528,512]{1,0:T(8,128)(2,1)S(1)}, bf16[528,512]{1,0:T(8,128)(2,1)S(1)}, u32[]{:S(2)}, u32[]{:S(2)}) collective-permute-start(bf16[528,512]{1,0:T(8,128)(2,1)S(1)} %pad_maximum_fusion), channel_id=1, source_target_pairs={{0,4},{2,6},{4,8},{6,10},{8,12},{10,14},{1,5},{3,7},{5,9},{7,11},{... | collective-permute-start | bytes 1622024 | tf_op jit(solution)/shard_map/ppermute | solution.py:128
  8.3 11.0 %collective-permute-start.2 = (s32[1,4]{1,0:T(1,128)S(1)}, s32[1,4]{1,0:T(1,128)S(1)}, u32[]{:S(2)}, u32[]{:S(2)}) collective-permute-start(s32[1,4]{1,0:T(1,128)S(1)} %copy-done.4), channel_id=1, source_target_pairs={{2,4},{4,2},{6,8},{8,6},{10,12},{12,10},{3,5},{5,3},{7,9},{9,7},{1... | collective-permute-start | bytes 56 | tf_op jit(solution)/shard_map/ppermute | solution.py:128
  21.2 13.1 %collective-permute-start.3 = (bf16[144,512]{1,0:T(8,128)(2,1)S(1)}, bf16[144,512]{1,0:T(8,128)(2,1)S(1)}, u32[]{:S(2)}, u32[]{:S(2)}) collective-permute-start(bf16[144,512]{1,0:T(8,128)(2,1)S(1)} %fusion.1), channel_id=1, source_target_pairs={{2,4},{4,2},{6,8},{8,6},{10,12},{12,10},{3,5},{5,3},{7,9},{9,7},{1... | collective-permute-start | bytes 442376 | tf_op jit(solution)/shard_map/ppermute | solution.py:128
  26.4 1.6 %copy-start = (bf16[512,2048]{1,0:T(8,128)(2,1)S(1)}, bf16[512,2048]{1,0:T(8,128)(2,1)}, u32[]{:S(2)}) copy-start(bf16[512,2048]{1,0:T(8,128)(2,1)} %q_ref.3) | copy-start | bytes 6291460

commit v2 on v1

v2 whole, which is shorter than its diff:
```python
import functools

import jax
import jax.numpy as jnp
from jax import lax
from jax.experimental import pallas as pl
from jax.experimental.pallas import tpu as pltpu
from jax.sharding import PartitionSpec as P

HD = 128
BLOCK = 128
RADIUS = 2
GROUP = 8
ROWS = 128
PAD = 16
SCALE = HD ** (-0.5) * 1.4426950408889634
HIDDEN = -1e30
NT = (((1,), (1,)), ((), ()))
NN = (((1,), (0,)), ((), ()))
VMEM = pl.BlockSpec(memory_space=pltpu.VMEM)
SMEM = pl.BlockSpec(memory_space=pltpu.SMEM)
HBM = pl.BlockSpec(memory_space=pltpu.HBM)
PARAMS = pltpu.CompilerParams(vmem_limit_bytes=24 << 20)


def column_of(row):
    return jnp.broadcast_to(row, (HD, row.shape[1])).T


def bias_of(query_level, key_level):
    wide = jnp.concatenate([query_level] * (key_level.shape[1] // HD), axis=1)
    return jnp.where(key_level <= wide, 0.0, HIDDEN)


def piece_kernel(where_ref, asked_ref, load_ref, piece_ref):
    tok = load_ref.shape[0] - PAD
    position = where_ref[0]
    odd = lax.rem(position, 2)
    entry = jnp.where(odd == 1, asked_ref[0, 1], asked_ref[0, 2])
    blocks = tok // BLOCK
    first = pl.multiple_of(jnp.clip(entry - position * blocks, 0, blocks - 1) * BLOCK, BLOCK)
    piece_ref[:BLOCK, :] = load_ref[pl.ds(first, BLOCK), :]
    level = load_ref[tok:, pl.ds(first, BLOCK)]
    piece_ref[BLOCK:, :] = jnp.concatenate([level] * (load_ref.shape[1] // BLOCK), axis=1)


def own_kernel(kv_heads, q_ref, load_ref, level_ref, o_ref, lse_ref, bias_ref, vx_ref):
    tok = q_ref.shape[0]
    level = level_ref[...].astype(jnp.float32)
    bias_ref[...] = bias_of(column_of(level), level)
    lane = lax.broadcasted_iota(jnp.int32, (ROWS, HD), 1)
    vx_ref[:, HD:] = jnp.ones((tok, HD), jnp.bfloat16)

    def step(g, carry):
        base = pl.multiple_of(g * (GROUP * HD), GROUP * HD)
        cols = pl.ds(pl.multiple_of(g * HD, HD), HD)
        vx_ref[:, :HD] = load_ref[:tok, pl.ds(pl.multiple_of((g + kv_heads) * HD, HD), HD)]
        for r in range(0, tok, ROWS):
            rows = pl.ds(r, ROWS)
            lse = jnp.zeros((ROWS, HD), jnp.float32)
            for h in range(GROUP):
                head = pl.ds(base + h * HD, HD)
                s = lax.dot_general(q_ref[rows, head], load_ref[:tok, cols], NT, preferred_element_type=jnp.float32)
                s = s * SCALE + bias_ref[rows, :]
                top = jnp.max(s, axis=1, keepdims=True)
                p = jnp.exp2(s - top).astype(jnp.bfloat16)
                o = lax.dot_general(p, vx_ref[...], NN, preferred_element_type=jnp.float32)
                total = o[:, HD:]
                o_ref[rows, head] = o[:, :HD] / total
                lse = jnp.where(lane == h, top + jnp.log2(total), lse)
            lse_ref[g, rows, :] = lse
        return carry

    lax.fori_loop(0, kv_heads, step, 0)


def far_kernel(
    kv_heads, where_ref, members_ref, q_ref, level_ref, o_ref, lse_ref, lo_ref, near_ref, diag_ref, hi_ref,
    out_ref, bias_ref, kx_ref, vx_ref, kl_ref, done_ref, sems,
):
    tok = q_ref.shape[0]
    far = kx_ref.shape[0]
    blocks = tok // BLOCK
    position = where_ref[0]
    odd = lax.rem(position, 2)
    before, after = members_ref[0, 1], members_ref[0, 2]
    near = jnp.where(odd == 1, before, after)
    diag = jnp.where(odd == 1, after, before)
    entries = (
        (lo_ref, members_ref[0, 0], position - 2),
        (near_ref, near, position + 1 - 2 * odd),
        (diag_ref, diag, None),
        (hi_ref, members_ref[0, 3], position + 2),
    )
    firsts = []
    for slot, (ref, entry, owner) in enumerate(entries):
        if owner is None:
            first = 0
            level = ref[BLOCK : BLOCK + 1, :BLOCK]
        else:
            first = pl.multiple_of(jnp.clip(entry - owner * blocks, 0, blocks - 1) * BLOCK, BLOCK)
            level = ref[tok : tok + 1, pl.ds(first, BLOCK)]
        firsts.append(first)
        level = jnp.where(entry >= 0, level.astype(jnp.float32), 1e9)
        kl_ref[0:1, slot * BLOCK : (slot + 1) * BLOCK] = level
    query_level = column_of(level_ref[...].astype(jnp.float32))
    bias_ref[...] = bias_of(query_level, kl_ref[0:1, :])
    vx_ref[:, HD:] = jnp.ones((far, HD), jnp.bfloat16)

    def out_copy(g, r):
        spot = (pl.ds(r, ROWS), pl.ds(pl.multiple_of(g * (GROUP * HD), GROUP * HD), GROUP * HD))
        return pltpu.make_async_copy(done_ref.at[spot], out_ref.at[spot], sems.at[g, r // ROWS])

    def step(g, carry):
        base = pl.multiple_of(g * (GROUP * HD), GROUP * HD)
        cols = pl.ds(pl.multiple_of(g * HD, HD), HD)
        vcols = pl.ds(pl.multiple_of((g + kv_heads) * HD, HD), HD)
        for slot, (ref, _, _) in enumerate(entries):
            picked = pl.ds(firsts[slot], BLOCK)
            kx_ref[slot * BLOCK : (slot + 1) * BLOCK, :] = ref[picked, cols]
            vx_ref[slot * BLOCK : (slot + 1) * BLOCK, :HD] = ref[picked, vcols]
        for r in range(0, tok, ROWS):
            rows = pl.ds(r, ROWS)
            lse = lse_ref[g, rows, :]
            for h in range(GROUP):
                head = pl.ds(base + h * HD, HD)
                own = lse[:, h : h + 1]
                s = lax.dot_general(q_ref[rows, head], kx_ref[...], NT, preferred_element_type=jnp.float32)
                s = s * SCALE + bias_ref[rows, :]
                top = jnp.maximum(jnp.max(s, axis=1, keepdims=True), own)
                p = jnp.exp2(s - top).astype(jnp.bfloat16)
                o = lax.dot_general(p, vx_ref[...], NN, preferred_element_type=jnp.float32)
                share = jnp.exp2(own - top)
                mixed = (o[:, :HD] + share * o_ref[rows, head]) / (o[:, HD:] + share)
                done_ref[rows, head] = mixed.astype(jnp.bfloat16)
            out_copy(g, r).start()
        return carry

    lax.fori_loop(0, kv_heads, step, 0)
    for g in range(kv_heads):
        for r in range(0, tok, ROWS):
            out_copy(g, r).wait()


def pairs_of(size, kind):
    if kind == "near":
        edges = [(i, i + 1) for i in range(0, size - 1, 2)]
        return [p for a, b in edges for p in ((a, b), (b, a))]
    if kind == "diag":
        edges = [(i, i + 1) for i in range(1, size - 1, 2)]
        return [p for a, b in edges for p in ((a, b), (b, a))]
    return [(i, i + kind) for i in range(size) if 0 <= i + kind < size]


def cost_of(tok, keys, heads):
    return pl.CostEstimate(
        flops=4 * tok * keys * heads * HD, transcendentals=tok * keys * heads, bytes_accessed=8 << 20
    )


def local(queries, keys, values, levels, members):
    tok = queries.shape[0]
    kv_heads = keys.shape[1] // HD
    heads = queries.shape[1] // HD
    size = lax.axis_size("seq")
    where = lax.axis_index("seq").astype(jnp.int32)[None]
    level_line = levels[None, :]
    send = lambda array, kind: lax.ppermute(array, "seq", pairs_of(size, kind))
    width = 2 * keys.shape[1]

    asked = send(members, "diag")
    level_rows = jnp.broadcast_to(level_line, (PAD, width)).astype(jnp.bfloat16)
    level_rows, asked = lax.optimization_barrier((level_rows, asked))
    load = jnp.concatenate([jnp.concatenate([keys, values], axis=1), level_rows], axis=0)
    from_hi = send(load, -2)
    from_lo = send(load, 2)
    from_near = send(load, "near")
    piece = pl.pallas_call(
        piece_kernel,
        in_specs=[SMEM, SMEM, VMEM],
        out_specs=VMEM,
        out_shape=jax.ShapeDtypeStruct((BLOCK + PAD, width), jnp.bfloat16),
        compiler_params=PARAMS,
        cost_estimate=pl.CostEstimate(flops=0, transcendentals=0, bytes_accessed=8 << 20),
    )(where, asked, load)
    from_diag = send(piece, "diag")

    part, lse = pl.pallas_call(
        functools.partial(own_kernel, kv_heads),
        in_specs=[VMEM] * 3,
        out_specs=[VMEM] * 2,
        out_shape=[
            jax.ShapeDtypeStruct((tok, heads * HD), jnp.float32),
            jax.ShapeDtypeStruct((kv_heads, tok, HD), jnp.float32),
        ],
        scratch_shapes=[pltpu.VMEM((tok, tok), jnp.float32), pltpu.VMEM((tok, 2 * HD), jnp.bfloat16)],
        compiler_params=PARAMS,
        cost_estimate=cost_of(tok, tok, heads),
    )(queries, load, level_line)

    far = 2 * RADIUS * BLOCK
    return pl.pallas_call(
        functools.partial(far_kernel, kv_heads),
        in_specs=[SMEM] * 2 + [VMEM] * 8,
        out_specs=HBM,
        scratch_shapes=[
            pltpu.VMEM((tok, far), jnp.float32),
            pltpu.VMEM((far, HD), jnp.bfloat16),
            pltpu.VMEM((far, 2 * HD), jnp.bfloat16),
            pltpu.VMEM((8, far), jnp.float32),
            pltpu.VMEM((tok, heads * HD), jnp.bfloat16),
            pltpu.SemaphoreType.DMA((kv_heads, tok // ROWS)),
        ],
        out_shape=jax.ShapeDtypeStruct((tok, heads * HD), jnp.bfloat16),
        compiler_params=PARAMS,
        cost_estimate=cost_of(tok, far, heads),
    )(where, members, queries, level_line, part, lse, from_lo, from_near, from_diag, from_hi)


def solution(mesh):
    placed = (
        P(("grp", "seq"), "head"),
        P(("grp", "seq"), "head"),
        P(("grp", "seq"), "head"),
        P(("grp", "seq")),
        P(("grp", "seq"), None),
    )
    return jax.shard_map(
        local, mesh=mesh, in_specs=placed, out_specs=P(("grp", "seq"), "head"), check_vma=False
    )
```

time: 43.2 us -> 44.7 us (1.035)
  the two profiles are of different devices: /device:TPU:10 before, /device:TPU:28 now
where the time goes in v2:
time: 44.7 us; the launch traced here: 44.5 us
  Pallas kernels  22.2 us (50%)
  starting transfers between devices  13.2 us (30%)
  waiting for transfers between devices  5.69 us (13%)
  other arithmetic  1.75 us (4%)
  local copies, waits for them, and re-layouts  1.6 us (4%)
    pallas_call x1, Pallas kernels, local(): pl.pallas_call(functools.partial(far_kernel, kv_heads), in_specs=[SMEM] *...  15.5 us
    ppermute x5, starting transfers between devices, local(): send = lambda array, kind: lax.ppermute(array, 'seq', pairs_of(size, kind))  13.2 us
    pallas_call x1, Pallas kernels, local(): pl.pallas_call(functools.partial(own_kernel, kv_heads), in_specs=[VMEM] *...  6.12 us
    ppermute x5, waiting for transfers between devices, local(): send = lambda array, kind: lax.ppermute(array, 'seq', pairs_of(size, kind))  5.69 us
    unnamed x6, local copies, waits for them, and re-layouts  1.59 us
    concatenate x1, other arithmetic, local(): jnp.concatenate([jnp.concatenate([keys, values], axis=1), level_rows], ax...  1.07 us
  transfers between devices with their start and end apart: 5, of which 2 were waited for; matrix products, arithmetic and copies ran while one was open for 2% of the time, Pallas kernels for 15%

profile of v2, /device:TPU:28, one launch (start us, length us, event | category | flops | bytes accessed | tf_op | source)
XLA Modules:
  0.0 44.5 jit_solution(4496225964231624261)
XLA Ops:
  0.0 0.0 copy-start.1
  0.0 3.4 %collective-permute-start = (s32[1,4]{1,0:T(1,128)}, s32[1,4]{1,0:T(1,128)S(1)}, u32[]{:S(2)}, u32[]{:S(2)}) collective-permute-start(s32[1,4]{1,0:T(1,128)} %members_ref.1), channel_id=1, source_target_pairs={{2,4},{4,2},{6,8},{8,6},{10,12},{12,10},{3,5},{5,3},{7,9},{9,7},{1... | collective-permute-start | bytes 56 | tf_op jit(solution)/shard_map/ppermute | solution.py:168
  3.4 0.7 %convert_element_type.4 = bf16[512]{0:T(512)(128)(2,1)S(1)} convert(s32[512]{0:T(512)} %param.8) | non-fusion elementwise | flops 512 | bytes 3072 | tf_op jit(solution)/shard_map/convert_element_type | solution.py:172
  4.1 2.5 %collective-permute-done.asked_ref = s32[1,4]{1,0:T(1,128)S(1)} collective-permute-done((s32[1,4]{1,0:T(1,128)}, s32[1,4]{1,0:T(1,128)S(1)}, u32[]{:S(2)}, u32[]{:S(2)}) %collective-permute-start) | collective-permute-done | bytes 48 | tf_op jit(solution)/shard_map/ppermute | solution.py:168
  6.6 1.1 %pad_maximum_fusion.load_ref = bf16[528,512]{1,0:T(8,128)(2,1)S(1)} fusion(bf16[16,512]{1,0:T(8,128)(2,1)S(1)} %broadcast_in_dim.13, bf16[512,256]{1,0:T(8,128)(2,1)} %param.7, bf16[512,256]{1,0:T(8,128)(2,1)} %param.6), kind=kLoop, calls=%fused_computation | loop fusion | flops 1622016 | bytes 1081344 | tf_op jit(solution)/shard_map/concatenate | solution.py:174
  7.7 2.4 %collective-permute-start.4 = (bf16[528,512]{1,0:T(8,128)(2,1)S(1)}, bf16[528,512]{1,0:T(8,128)(2,1)S(1)}, u32[]{:S(2)}, u32[]{:S(2)}) collective-permute-start(bf16[528,512]{1,0:T(8,128)(2,1)S(1)} %pad_maximum_fusion.load_ref), channel_id=1, source_target_pairs={{4,0},{6,2},{8,4},{10,6},{12,8},{14,10},{5,1},{7,3},{9,5},{11,7},{... | collective-permute-start | bytes 1622024 | tf_op jit(solution)/shard_map/ppermute | solution.py:168
  10.1 1.6 %collective-permute-start.2 = (bf16[528,512]{1,0:T(8,128)(2,1)S(1)}, bf16[528,512]{1,0:T(8,128)(2,1)S(1)}, u32[]{:S(2)}, u32[]{:S(2)}) collective-permute-start(bf16[528,512]{1,0:T(8,128)(2,1)S(1)} %pad_maximum_fusion.load_ref), channel_id=1, source_target_pairs={{0,2},{2,0},{4,6},{6,4},{8,10},{10,8},{12,14},{14,12},{1,3},{3,1},... | collective-permute-start | bytes 1622024 | tf_op jit(solution)/shard_map/ppermute | solution.py:168
  11.6 1.3 %collective-permute-start.1 = (bf16[528,512]{1,0:T(8,128)(2,1)S(1)}, bf16[528,512]{1,0:T(8,128)(2,1)S(1)}, u32[]{:S(2)}, u32[]{:S(2)}) collective-permute-start(bf16[528,512]{1,0:T(8,128)(2,1)S(1)} %pad_maximum_fusion.load_ref), channel_id=1, source_target_pairs={{0,4},{2,6},{4,8},{6,10},{8,12},{10,14},{1,5},{3,7},{5,9},{7,11},{... | collective-permute-start | bytes 1622024 | tf_op jit(solution)/shard_map/ppermute | solution.py:168
  12.9 0.6 %shard_map.56 = bf16[144,512]{1,0:T(8,128)(2,1)S(1)} custom-call(s32[1]{0:T(128)} %bitcast.where_ref, s32[1,4]{1,0:T(1,128)S(1)} %collective-permute-done.asked_ref, bf16[528,512]{1,0:T(8,128)(2,1)S(1)} %pad_maximum_fusion.load_ref), custom_call_target="tpu_custom_call" | custom-call | bytes 8388608 | tf_op jit(solution)/shard_map/pallas_call | solution.py:178
  13.5 4.5 %collective-permute-start.3 = (bf16[144,512]{1,0:T(8,128)(2,1)S(1)}, bf16[144,512]{1,0:T(8,128)(2,1)S(1)}, u32[]{:S(2)}, u32[]{:S(2)}) collective-permute-start(bf16[144,512]{1,0:T(8,128)(2,1)S(1)} %shard_map.56), channel_id=1, source_target_pairs={{2,4},{4,2},{6,8},{8,6},{10,12},{12,10},{3,5},{5,3},{7,9},{9,7},{1... | collective-permute-start | bytes 442376 | tf_op jit(solution)/shard_map/ppermute | solution.py:168
  18.0 0.0 copy-done.1
  18.0 0.0 copy-start
  18.0 1.6 %copy-done = bf16[512,2048]{1,0:T(8,128)(2,1)S(1)} copy-done((bf16[512,2048]{1,0:T(8,128)(2,1)S(1)}, bf16[512,2048]{1,0:T(8,128)(2,1)}, u32[]{:S(2)}) %copy-start) | copy-done | bytes 2097176
  19.6 0.0 copy-start.2
  19.6 6.1 %shard_map.55 = (f32[512,2048]{1,0:T(8,128)S(1)}, f32[2,512,128]{2,1,0:T(8,128)S(1)}) custom-call(bf16[512,2048]{1,0:T(8,128)(2,1)S(1)} %copy-done, bf16[528,512]{1,0:T(8,128)(2,1)S(1)} %pad_maximum_fusion.load_ref, s32[1,512]{1,0:T(1,128)S(1)} %bitcast.2), custom_call_target="tpu_custom_call" | custom-call | flops 2147483648 | bytes 8388608 | tf_op jit(solution)/shard_map/pallas_call | solution.py:188
  25.7 3.2 %collective-permute-done.3.diag_ref = bf16[144,512]{1,0:T(8,128)(2,1)S(1)} collective-permute-done((bf16[144,512]{1,0:T(8,128)(2,1)S(1)}, bf16[144,512]{1,0:T(8,128)(2,1)S(1)}, u32[]{:S(2)}, u32[]{:S(2)}) %collective-permute-start.3) | collective-permute-done | bytes 147488 | tf_op jit(solution)/shard_map/ppermute | solution.py:168
  28.9 0.0 collective-permute-done.4.hi_ref
  28.9 0.0 collective-permute-done.2.near_ref
  28.9 0.0 collective-permute-done.1.lo_ref
  29.0 0.0 copy-done.2
  29.0 15.5 %shard_map.57 = bf16[512,2048]{1,0:T(8,128)(2,1)} custom-call(s32[1]{0:T(128)} %bitcast.where_ref, s32[1,4]{1,0:T(1,128)S(1)} %copy-done.2, bf16[512,2048]{1,0:T(8,128)(2,1)S(1)} %copy-done, s32[1,512]{1,0:T(1,128)S(1)} %bitcast.3, f32[512,2048]{1,0:T(8,128)S(1)} %get-tuple-element.10.o_ref, f32[2,512,128]{2,1,0:T(8,128)S(1)} %get-tuple-element.11.lse_ref, ...), custom_call_target="tpu_custom_call" | custom-call | flops 2147483648 | bytes 8388608 | tf_op jit(solution)/shard_map/pallas_call | solution.py:202
  (1 shorter events, 0.0 us)
Async XLA Ops:
  0.0 18.0 %copy-start.1 = (s32[512]{0:T(512)S(1)}, s32[512]{0:T(512)}, u32[]{:S(2)}) copy-start(s32[512]{0:T(512)} %param.8) | copy-start | bytes 6148
  0.0 6.6 %collective-permute-start = (s32[1,4]{1,0:T(1,128)}, s32[1,4]{1,0:T(1,128)S(1)}, u32[]{:S(2)}, u32[]{:S(2)}) collective-permute-start(s32[1,4]{1,0:T(1,128)} %members_ref.1), channel_id=1, source_target_pairs={{2,4},{4,2},{6,8},{8,6},{10,12},{12,10},{3,5},{5,3},{7,9},{9,7},{1... | collective-permute-start | bytes 56 | tf_op jit(solution)/shard_map/ppermute | solution.py:168
  7.7 21.3 %collective-permute-start.4 = (bf16[528,512]{1,0:T(8,128)(2,1)S(1)}, bf16[528,512]{1,0:T(8,128)(2,1)S(1)}, u32[]{:S(2)}, u32[]{:S(2)}) collective-permute-start(bf16[528,512]{1,0:T(8,128)(2,1)S(1)} %pad_maximum_fusion.load_ref), channel_id=1, source_target_pairs={{4,0},{6,2},{8,4},{10,6},{12,8},{14,10},{5,1},{7,3},{9,5},{11,7},{... | collective-permute-start | bytes 1622024 | tf_op jit(solution)/shard_map/ppermute | solution.py:168
  10.1 18.9 %collective-permute-start.2 = (bf16[528,512]{1,0:T(8,128)(2,1)S(1)}, bf16[528,512]{1,0:T(8,128)(2,1)S(1)}, u32[]{:S(2)}, u32[]{:S(2)}) collective-permute-start(bf16[528,512]{1,0:T(8,128)(2,1)S(1)} %pad_maximum_fusion.load_ref), channel_id=1, source_target_pairs={{0,2},{2,0},{4,6},{6,4},{8,10},{10,8},{12,14},{14,12},{1,3},{3,1},... | collective-permute-start | bytes 1622024 | tf_op jit(solution)/shard_map/ppermute | solution.py:168
  11.6 17.3 %collective-permute-start.1 = (bf16[528,512]{1,0:T(8,128)(2,1)S(1)}, bf16[528,512]{1,0:T(8,128)(2,1)S(1)}, u32[]{:S(2)}, u32[]{:S(2)}) collective-permute-start(bf16[528,512]{1,0:T(8,128)(2,1)S(1)} %pad_maximum_fusion.load_ref), channel_id=1, source_target_pairs={{0,4},{2,6},{4,8},{6,10},{8,12},{10,14},{1,5},{3,7},{5,9},{7,11},{... | collective-permute-start | bytes 1622024 | tf_op jit(solution)/shard_map/ppermute | solution.py:168
  13.5 15.5 %collective-permute-start.3 = (bf16[144,512]{1,0:T(8,128)(2,1)S(1)}, bf16[144,512]{1,0:T(8,128)(2,1)S(1)}, u32[]{:S(2)}, u32[]{:S(2)}) collective-permute-start(bf16[144,512]{1,0:T(8,128)(2,1)S(1)} %shard_map.56), channel_id=1, source_target_pairs={{2,4},{4,2},{6,8},{8,6},{10,12},{12,10},{3,5},{5,3},{7,9},{9,7},{1... | collective-permute-start | bytes 442376 | tf_op jit(solution)/shard_map/ppermute | solution.py:168
  18.0 1.6 %copy-start = (bf16[512,2048]{1,0:T(8,128)(2,1)S(1)}, bf16[512,2048]{1,0:T(8,128)(2,1)}, u32[]{:S(2)}) copy-start(bf16[512,2048]{1,0:T(8,128)(2,1)} %q_ref.3) | copy-start | bytes 6291460
  19.6 9.3 %copy-start.2 = (s32[1,4]{1,0:T(1,128)S(1)}, s32[1,4]{1,0:T(1,128)}, u32[]{:S(2)}) copy-start(s32[1,4]{1,0:T(1,128)} %members_ref.1) | copy-start | bytes 52

commit v3 on v2

--- a/solution.py
+++ b/solution.py
@@ -44,20 +44,27 @@
     piece_ref[BLOCK:, :] = jnp.concatenate([level] * (load_ref.shape[1] // BLOCK), axis=1)
 
 
-def own_kernel(kv_heads, q_ref, load_ref, level_ref, o_ref, lse_ref, bias_ref, vx_ref):
+def own_kernel(kv_heads, q_hbm, load_ref, o_ref, lse_ref, q_ref, column_ref, bias_ref, vx_ref, sems):
     tok = q_ref.shape[0]
-    level = level_ref[...].astype(jnp.float32)
-    bias_ref[...] = bias_of(column_of(level), level)
-    lane = lax.broadcasted_iota(jnp.int32, (ROWS, HD), 1)
+
+    def q_copy(g):
+        spot = (pl.ds(0, tok), pl.ds(pl.multiple_of(g * (GROUP * HD), GROUP * HD), GROUP * HD))
+        return pltpu.make_async_copy(q_hbm.at[spot], q_ref.at[spot], sems.at[g])
+
+    for g in range(kv_heads):
+        q_copy(g).start()
+    level = load_ref[tok : tok + 1, :].astype(jnp.float32)
+    column_ref[...] = column_of(level)
+    bias_ref[...] = bias_of(column_ref[...], level)
     vx_ref[:, HD:] = jnp.ones((tok, HD), jnp.bfloat16)
 
     def step(g, carry):
         base = pl.multiple_of(g * (GROUP * HD), GROUP * HD)
         cols = pl.ds(pl.multiple_of(g * HD, HD), HD)
+        q_copy(g).wait()
         vx_ref[:, :HD] = load_ref[:tok, pl.ds(pl.multiple_of((g + kv_heads) * HD, HD), HD)]
         for r in range(0, tok, ROWS):
             rows = pl.ds(r, ROWS)
-            lse = jnp.zeros((ROWS, HD), jnp.float32)
             for h in range(GROUP):
                 head = pl.ds(base + h * HD, HD)
                 s = lax.dot_general(q_ref[rows, head], load_ref[:tok, cols], NT, preferred_element_type=jnp.float32)
@@ -67,15 +74,14 @@
                 o = lax.dot_general(p, vx_ref[...], NN, preferred_element_type=jnp.float32)
                 total = o[:, HD:]
                 o_ref[rows, head] = o[:, :HD] / total
-                lse = jnp.where(lane == h, top + jnp.log2(total), lse)
-            lse_ref[g, rows, :] = lse
+                lse_ref[rows, head] = top + jnp.log2(total)
         return carry
 
     lax.fori_loop(0, kv_heads, step, 0)
 
 
 def far_kernel(
-    kv_heads, where_ref, members_ref, q_ref, level_ref, o_ref, lse_ref, lo_ref, near_ref, diag_ref, hi_ref,
+    kv_heads, where_ref, members_ref, q_ref, column_ref, o_ref, lse_ref, lo_ref, near_ref, diag_ref, hi_ref,
     out_ref, bias_ref, kx_ref, vx_ref, kl_ref, done_ref, sems,
 ):
     tok = q_ref.shape[0]
@@ -84,13 +90,17 @@
     position = where_ref[0]
     odd = lax.rem(position, 2)
     before, after = members_ref[0, 1], members_ref[0, 2]
+    flip = lax.rem(lax.div(position, 2), 2) == 1
+    lowest, highest = members_ref[0, 0], members_ref[0, 3]
+    even, even_owner = jnp.where(flip, lowest, highest), position + jnp.where(flip, -2, 2)
+    other, other_owner = jnp.where(flip, highest, lowest), position + jnp.where(flip, 2, -2)
     near = jnp.where(odd == 1, before, after)
     diag = jnp.where(odd == 1, after, before)
     entries = (
-        (lo_ref, members_ref[0, 0], position - 2),
+        (lo_ref, other, other_owner),
         (near_ref, near, position + 1 - 2 * odd),
         (diag_ref, diag, None),
-        (hi_ref, members_ref[0, 3], position + 2),
+        (hi_ref, even, even_owner),
     )
     firsts = []
     for slot, (ref, entry, owner) in enumerate(entries):
@@ -103,8 +113,7 @@
         firsts.append(first)
         level = jnp.where(entry >= 0, level.astype(jnp.float32), 1e9)
         kl_ref[0:1, slot * BLOCK : (slot + 1) * BLOCK] = level
-    query_level = column_of(level_ref[...].astype(jnp.float32))
-    bias_ref[...] = bias_of(query_level, kl_ref[0:1, :])
+    bias_ref[...] = bias_of(column_ref[...], kl_ref[0:1, :])
     vx_ref[:, HD:] = jnp.ones((far, HD), jnp.bfloat16)
 
     def out_copy(g, r):
@@ -121,13 +130,13 @@
             vx_ref[slot * BLOCK : (slot + 1) * BLOCK, :HD] = ref[picked, vcols]
         for r in range(0, tok, ROWS):
             rows = pl.ds(r, ROWS)
-            lse = lse_ref[g, rows, :]
             for h in range(GROUP):
                 head = pl.ds(base + h * HD, HD)
-                own = lse[:, h : h + 1]
+                own = lse_ref[rows, head]
                 s = lax.dot_general(q_ref[rows, head], kx_ref[...], NT, preferred_element_type=jnp.float32)
                 s = s * SCALE + bias_ref[rows, :]
-                top = jnp.maximum(jnp.max(s, axis=1, keepdims=True), own)
+                tops = [s[:, i : i + HD] for i in range(0, far, HD)]
+                top = jnp.max(functools.reduce(jnp.maximum, tops, own), axis=1, keepdims=True)
                 p = jnp.exp2(s - top).astype(jnp.bfloat16)
                 o = lax.dot_general(p, vx_ref[...], NN, preferred_element_type=jnp.float32)
                 share = jnp.exp2(own - top)
@@ -149,7 +158,8 @@
     if kind == "diag":
         edges = [(i, i + 1) for i in range(1, size - 1, 2)]
         return [p for a, b in edges for p in ((a, b), (b, a))]
-    return [(i, i + kind) for i in range(size) if 0 <= i + kind < size]
+    edges = [(i, i + 2) for i in range(size - 2) if (i // 2) % 2 == (kind == "odd")]
+    return [p for a, b in edges for p in ((a, b), (b, a))]
 
 
 def cost_of(tok, keys, heads):
@@ -170,10 +180,10 @@
 
     asked = send(members, "diag")
     level_rows = jnp.broadcast_to(level_line, (PAD, width)).astype(jnp.bfloat16)
-    level_rows, asked = lax.optimization_barrier((level_rows, asked))
     load = jnp.concatenate([jnp.concatenate([keys, values], axis=1), level_rows], axis=0)
-    from_hi = send(load, -2)
-    from_lo = send(load, 2)
+    load, asked = lax.optimization_barrier((load, asked))
+    from_hi = send(load, "even")
+    from_lo = send(load, "odd")
     from_near = send(load, "near")
     piece = pl.pallas_call(
         piece_kernel,
@@ -185,18 +195,24 @@
     )(where, asked, load)
     from_diag = send(piece, "diag")
 
-    part, lse = pl.pallas_call(
+    part, lse, rows_in, column = pl.pallas_call(
         functools.partial(own_kernel, kv_heads),
-        in_specs=[VMEM] * 3,
-        out_specs=[VMEM] * 2,
+        in_specs=[HBM, VMEM],
+        out_specs=[VMEM] * 4,
         out_shape=[
             jax.ShapeDtypeStruct((tok, heads * HD), jnp.float32),
-            jax.ShapeDtypeStruct((kv_heads, tok, HD), jnp.float32),
+            jax.ShapeDtypeStruct((tok, heads * HD), jnp.float32),
+            jax.ShapeDtypeStruct((tok, heads * HD), jnp.bfloat16),
+            jax.ShapeDtypeStruct((tok, HD), jnp.float32),
         ],
-        scratch_shapes=[pltpu.VMEM((tok, tok), jnp.float32), pltpu.VMEM((tok, 2 * HD), jnp.bfloat16)],
+        scratch_shapes=[
+            pltpu.VMEM((tok, tok), jnp.float32),
+            pltpu.VMEM((tok, 2 * HD), jnp.bfloat16),
+            pltpu.SemaphoreType.DMA((kv_heads,)),
+        ],
         compiler_params=PARAMS,
         cost_estimate=cost_of(tok, tok, heads),
-    )(queries, load, level_line)
+    )(pltpu.with_memory_space_constraint(queries, pltpu.HBM), load)
 
     far = 2 * RADIUS * BLOCK
     return pl.pallas_call(
@@ -214,7 +230,7 @@
         out_shape=jax.ShapeDtypeStruct((tok, heads * HD), jnp.bfloat16),
         compiler_params=PARAMS,
         cost_estimate=cost_of(tok, far, heads),
-    )(where, members, queries, level_line, part, lse, from_lo, from_near, from_diag, from_hi)
+    )(where, members, rows_in, column, part, lse, from_lo, from_near, from_diag, from_hi)
 
 
 def solution(mesh):

time: 44.7 us -> 35.5 us (0.79)
  the two profiles are of different devices: /device:TPU:28 before, /device:TPU:16 now
where the time goes in v3:
time: 35.5 us; the launch traced here: 35.3 us
  Pallas kernels  16.2 us (46%)
  starting transfers between devices  12.1 us (34%)
  waiting for transfers between devices  5.18 us (15%)
  other arithmetic  1.75 us (5%)
    ppermute x5, starting transfers between devices, local(): send = lambda array, kind: lax.ppermute(array, 'seq', pairs_of(size, kind))  12.1 us
    pallas_call x1, Pallas kernels, local(): pl.pallas_call(functools.partial(far_kernel, kv_heads), in_specs=[SMEM] *...  8.46 us
    pallas_call x1, Pallas kernels, local(): pl.pallas_call(functools.partial(own_kernel, kv_heads), in_specs=[HBM, VM...  7.14 us
    ppermute x5, waiting for transfers between devices, local(): send = lambda array, kind: lax.ppermute(array, 'seq', pairs_of(size, kind))  5.18 us
    concatenate x1, other arithmetic, local(): jnp.concatenate([jnp.concatenate([keys, values], axis=1), level_rows], ax...  1.06 us
  transfers between devices with their start and end apart: 5, of which 2 were waited for; matrix products, arithmetic and copies ran while one was open for 5% of the time, Pallas kernels for 22%

profile of v3, /device:TPU:16, one launch (start us, length us, event | category | flops | bytes accessed | tf_op | source)
XLA Modules:
  0.0 35.3 jit_solution(7998561652796045995)
XLA Ops:
  0.0 3.3 %collective-permute-start = (s32[1,4]{1,0:T(1,128)}, s32[1,4]{1,0:T(1,128)S(1)}, u32[]{:S(2)}, u32[]{:S(2)}) collective-permute-start(s32[1,4]{1,0:T(1,128)} %members_ref.1), channel_id=1, source_target_pairs={{2,4},{4,2},{6,8},{8,6},{10,12},{12,10},{3,5},{5,3},{7,9},{9,7},{1... | collective-permute-start | bytes 56 | tf_op jit(solution)/shard_map/ppermute | solution.py:178
  3.3 0.7 %convert_element_type.4 = bf16[512]{0:T(512)(128)(2,1)S(1)} convert(s32[512]{0:T(512)} %param.8) | non-fusion elementwise | flops 512 | bytes 3072 | tf_op jit(solution)/shard_map/convert_element_type | solution.py:182
  4.0 1.1 %pad_maximum_fusion.load_ref = bf16[528,512]{1,0:T(8,128)(2,1)S(1)} fusion(bf16[16,512]{1,0:T(8,128)(2,1)S(1)} %broadcast_in_dim.10, bf16[512,256]{1,0:T(8,128)(2,1)} %param.7, bf16[512,256]{1,0:T(8,128)(2,1)} %param.6), kind=kLoop, calls=%fused_computation | loop fusion | flops 1622016 | bytes 1081344 | tf_op jit(solution)/shard_map/concatenate | solution.py:183
  5.0 1.4 %collective-permute-done.asked_ref = s32[1,4]{1,0:T(1,128)S(1)} collective-permute-done((s32[1,4]{1,0:T(1,128)}, s32[1,4]{1,0:T(1,128)S(1)}, u32[]{:S(2)}, u32[]{:S(2)}) %collective-permute-start) | collective-permute-done | bytes 48 | tf_op jit(solution)/shard_map/ppermute | solution.py:178
  6.5 1.6 %collective-permute-start.4 = (bf16[528,512]{1,0:T(8,128)(2,1)S(1)}, bf16[528,512]{1,0:T(8,128)(2,1)S(1)}, u32[]{:S(2)}, u32[]{:S(2)}) collective-permute-start(bf16[528,512]{1,0:T(8,128)(2,1)S(1)} %pad_maximum_fusion.load_ref), channel_id=1, source_target_pairs={{0,4},{4,0},{2,6},{6,2},{8,12},{12,8},{10,14},{14,10},{1,5},{5,1},... | collective-permute-start | bytes 1622024 | tf_op jit(solution)/shard_map/ppermute | solution.py:178
  8.0 0.0 collective-permute-start.2
  8.0 2.7 %collective-permute-start.1 = (bf16[528,512]{1,0:T(8,128)(2,1)S(1)}, bf16[528,512]{1,0:T(8,128)(2,1)S(1)}, u32[]{:S(2)}, u32[]{:S(2)}) collective-permute-start(bf16[528,512]{1,0:T(8,128)(2,1)S(1)} %pad_maximum_fusion.load_ref), channel_id=1, source_target_pairs={{4,8},{8,4},{6,10},{10,6},{5,9},{9,5},{7,11},{11,7},{20,24},{24,20... | collective-permute-start | bytes 1622024 | tf_op jit(solution)/shard_map/ppermute | solution.py:178
  10.8 0.6 %shard_map.56 = bf16[144,512]{1,0:T(8,128)(2,1)S(1)} custom-call(s32[1]{0:T(128)} %bitcast.where_ref, s32[1,4]{1,0:T(1,128)S(1)} %collective-permute-done.asked_ref, bf16[528,512]{1,0:T(8,128)(2,1)S(1)} %pad_maximum_fusion.load_ref), custom_call_target="tpu_custom_call" | custom-call | bytes 8388608 | tf_op jit(solution)/shard_map/pallas_call | solution.py:188
  11.3 0.0 copy-start
  11.3 4.6 %collective-permute-start.3 = (bf16[144,512]{1,0:T(8,128)(2,1)S(1)}, bf16[144,512]{1,0:T(8,128)(2,1)S(1)}, u32[]{:S(2)}, u32[]{:S(2)}) collective-permute-start(bf16[144,512]{1,0:T(8,128)(2,1)S(1)} %shard_map.56), channel_id=1, source_target_pairs={{2,4},{4,2},{6,8},{8,6},{10,12},{12,10},{3,5},{5,3},{7,9},{9,7},{1... | collective-permute-start | bytes 442376 | tf_op jit(solution)/shard_map/ppermute | solution.py:178
  15.9 7.1 %shard_map.55 = (f32[512,2048]{1,0:T(8,128)S(1)}, f32[512,2048]{1,0:T(8,128)S(1)}, bf16[512,2048]{1,0:T(8,128)(2,1)S(1)}, f32[512,128]{1,0:T(8,128)S(1)}) custom-call(bf16[512,2048]{1,0:T(8,128)(2,1)} %q_hbm.1, bf16[528,512]{1,0:T(8,128)(2,1)S(1)} %pad_maximum_fusion.load_ref), custom_call_target="tpu_custom_call" | custom-call | flops 2147483648 | bytes 8388608 | tf_op jit(solution)/shard_map/pallas_call | solution.py:198
  23.1 3.8 %collective-permute-done.3.diag_ref = bf16[144,512]{1,0:T(8,128)(2,1)S(1)} collective-permute-done((bf16[144,512]{1,0:T(8,128)(2,1)S(1)}, bf16[144,512]{1,0:T(8,128)(2,1)S(1)}, u32[]{:S(2)}, u32[]{:S(2)}) %collective-permute-start.3) | collective-permute-done | bytes 147488 | tf_op jit(solution)/shard_map/ppermute | solution.py:178
  26.8 0.0 collective-permute-done.4.hi_ref
  26.8 0.0 collective-permute-done.2.near_ref
  26.9 0.0 collective-permute-done.1.lo_ref
  26.9 0.0 copy-done
  26.9 8.5 %shard_map.57 = bf16[512,2048]{1,0:T(8,128)(2,1)} custom-call(s32[1]{0:T(128)} %bitcast.where_ref, s32[1,4]{1,0:T(1,128)S(1)} %copy-done, bf16[512,2048]{1,0:T(8,128)(2,1)S(1)} %get-tuple-element.12.q_ref, f32[512,128]{1,0:T(8,128)S(1)} %get-tuple-element.13.column_ref, f32[512,2048]{1,0:T(8,128)S(1)} %get-tuple-element.14.o_ref, ...), custom_call_target="tpu_custom_call" | custom-call | flops 2147483648 | bytes 8388608 | tf_op jit(solution)/shard_map/pallas_call | solution.py:218
  (1 shorter events, 0.0 us)
Async XLA Ops:
  0.0 6.5 %collective-permute-start = (s32[1,4]{1,0:T(1,128)}, s32[1,4]{1,0:T(1,128)S(1)}, u32[]{:S(2)}, u32[]{:S(2)}) collective-permute-start(s32[1,4]{1,0:T(1,128)} %members_ref.1), channel_id=1, source_target_pairs={{2,4},{4,2},{6,8},{8,6},{10,12},{12,10},{3,5},{5,3},{7,9},{9,7},{1... | collective-permute-start | bytes 56 | tf_op jit(solution)/shard_map/ppermute | solution.py:178
  6.5 20.4 %collective-permute-start.4 = (bf16[528,512]{1,0:T(8,128)(2,1)S(1)}, bf16[528,512]{1,0:T(8,128)(2,1)S(1)}, u32[]{:S(2)}, u32[]{:S(2)}) collective-permute-start(bf16[528,512]{1,0:T(8,128)(2,1)S(1)} %pad_maximum_fusion.load_ref), channel_id=1, source_target_pairs={{0,4},{4,0},{2,6},{6,2},{8,12},{12,8},{10,14},{14,10},{1,5},{5,1},... | collective-permute-start | bytes 1622024 | tf_op jit(solution)/shard_map/ppermute | solution.py:178
  8.0 18.8 %collective-permute-start.2 = (bf16[528,512]{1,0:T(8,128)(2,1)S(1)}, bf16[528,512]{1,0:T(8,128)(2,1)S(1)}, u32[]{:S(2)}, u32[]{:S(2)}) collective-permute-start(bf16[528,512]{1,0:T(8,128)(2,1)S(1)} %pad_maximum_fusion.load_ref), channel_id=1, source_target_pairs={{0,2},{2,0},{4,6},{6,4},{8,10},{10,8},{12,14},{14,12},{1,3},{3,1},... | collective-permute-start | bytes 1622024 | tf_op jit(solution)/shard_map/ppermute | solution.py:178
  8.0 18.8 %collective-permute-start.1 = (bf16[528,512]{1,0:T(8,128)(2,1)S(1)}, bf16[528,512]{1,0:T(8,128)(2,1)S(1)}, u32[]{:S(2)}, u32[]{:S(2)}) collective-permute-start(bf16[528,512]{1,0:T(8,128)(2,1)S(1)} %pad_maximum_fusion.load_ref), channel_id=1, source_target_pairs={{4,8},{8,4},{6,10},{10,6},{5,9},{9,5},{7,11},{11,7},{20,24},{24,20... | collective-permute-start | bytes 1622024 | tf_op jit(solution)/shard_map/ppermute | solution.py:178
  11.3 15.5 %copy-start = (s32[1,4]{1,0:T(1,128)S(1)}, s32[1,4]{1,0:T(1,128)}, u32[]{:S(2)}) copy-start(s32[1,4]{1,0:T(1,128)} %members_ref.1) | copy-start | bytes 52
  11.3 15.5 %collective-permute-start.3 = (bf16[144,512]{1,0:T(8,128)(2,1)S(1)}, bf16[144,512]{1,0:T(8,128)(2,1)S(1)}, u32[]{:S(2)}, u32[]{:S(2)}) collective-permute-start(bf16[144,512]{1,0:T(8,128)(2,1)S(1)} %shard_map.56), channel_id=1, source_target_pairs={{2,4},{4,2},{6,8},{8,6},{10,12},{12,10},{3,5},{5,3},{7,9},{9,7},{1... | collective-permute-start | bytes 442376 | tf_op jit(solution)/shard_map/ppermute | solution.py:178

commit v4 on v2

v4 whole, which is shorter than its diff:
```python
import functools

import jax
import jax.numpy as jnp
from jax import lax
from jax.experimental import pallas as pl
from jax.experimental.pallas import tpu as pltpu
from jax.sharding import PartitionSpec as P

HD = 128
BLOCK = 128
GROUP = 8
ROWS = 256
PAD = 16
EARLY = 2
PICKED = ("even", "odd", "near", "diag")
SOURCES = ("even", "near", "odd", "diag")
SCALE = HD ** (-0.5) * 1.4426950408889634
HIDDEN = -1e30
NT = (((1,), (1,)), ((), ()))
NN = (((1,), (0,)), ((), ()))
VMEM = pl.BlockSpec(memory_space=pltpu.VMEM)
SMEM = pl.BlockSpec(memory_space=pltpu.SMEM)
HBM = pl.BlockSpec(memory_space=pltpu.HBM)
PARAMS = pltpu.CompilerParams(vmem_limit_bytes=24 << 20)


def column_of(row):
    return jnp.broadcast_to(row, (HD, row.shape[1])).T


def bias_of(query_level, key_level):
    wide = jnp.concatenate([query_level] * (key_level.shape[1] // HD), axis=1)
    return jnp.where(key_level <= wide, 0.0, HIDDEN)


def attend_own(kv_heads, chosen, q_ref, load_ref, acc_ref, top_ref, bias_ref, vx_ref):
    tok = q_ref.shape[0]
    vx_ref[:, HD:] = jnp.ones((tok, HD), jnp.bfloat16)
    for g in range(kv_heads):
        mine = [h for h in chosen if h // GROUP == g]
        if not mine:
            continue
        keys = load_ref[:tok, g * HD : (g + 1) * HD]
        vx_ref[:, :HD] = load_ref[:tok, (g + kv_heads) * HD : (g + kv_heads + 1) * HD]
        for r in range(0, tok, ROWS):
            rows = pl.ds(r, ROWS)
            for h in mine:
                spot = pl.ds((h - chosen[0]) * HD, HD)
                s = lax.dot_general(
                    q_ref[rows, h * HD : (h + 1) * HD], keys, NT, preferred_element_type=jnp.float32
                )
                s = s * SCALE + bias_ref[rows, :]
                top = jnp.max(s, axis=1, keepdims=True)
                p = jnp.exp2(s - top).astype(jnp.bfloat16)
                o = lax.dot_general(p, vx_ref[...], NN, preferred_element_type=jnp.float32)
                total = o[:, HD:]
                acc_ref[rows, spot] = o[:, :HD] / total
                top_ref[rows, spot] = top + jnp.log2(total)


def pack_kernel(
    kv_heads, k_hbm, v_hbm, q_hbm, level_hbm, load_ref, q_ref, column_ref, acc_ref, top_ref,
    level_ref, bias_ref, vx_ref, sems,
):
    tok, width = k_hbm.shape
    early = EARLY * HD
    rest = q_hbm.shape[1] - early
    copies = [
        pltpu.make_async_copy(level_hbm, level_ref, sems.at[0]),
        pltpu.make_async_copy(k_hbm, load_ref.at[pl.ds(0, tok), pl.ds(0, width)], sems.at[1]),
        pltpu.make_async_copy(v_hbm, load_ref.at[pl.ds(0, tok), pl.ds(width, width)], sems.at[2]),
        pltpu.make_async_copy(q_hbm.at[:, pl.ds(0, early)], q_ref.at[:, pl.ds(0, early)], sems.at[3]),
        pltpu.make_async_copy(q_hbm.at[:, pl.ds(early, rest)], q_ref.at[:, pl.ds(early, rest)], sems.at[4]),
    ]
    for copy in copies:
        copy.start()
    copies[0].wait()
    level = level_ref[...].astype(jnp.float32)
    load_ref[tok:, :] = jnp.broadcast_to(level, (PAD, tok)).astype(jnp.bfloat16)
    column_ref[...] = column_of(level)
    bias_ref[...] = bias_of(column_ref[...], level)
    for copy in copies[1:4]:
        copy.wait()
    attend_own(kv_heads, range(EARLY), q_ref, load_ref, acc_ref, top_ref, bias_ref, vx_ref)
    copies[4].wait()


def piece_kernel(sources, where_ref, *refs):
    count = len(sources)
    load_ref = refs[count]
    tok = load_ref.shape[0] - PAD
    position = where_ref[0]
    blocks = tok // BLOCK
    for source, asked_ref, piece_ref in zip(sources, refs[:count], refs[count + 1 :]):
        entry = asked_ref[0, partner_of(source, position)[2]]
        first = pl.multiple_of(jnp.clip(entry - position * blocks, 0, blocks - 1) * BLOCK, BLOCK)
        piece_ref[:BLOCK, :] = load_ref[pl.ds(first, BLOCK), :]
        level = load_ref[tok:, pl.ds(first, BLOCK)]
        piece_ref[BLOCK:, :] = jnp.concatenate([level] * (load_ref.shape[1] // BLOCK), axis=1)


def own_kernel(kv_heads, q_ref, load_ref, column_ref, acc_ref, top_ref, bias_ref, vx_ref):
    tok = q_ref.shape[0]
    bias_ref[...] = bias_of(column_ref[...], load_ref[tok : tok + 1, :].astype(jnp.float32))
    late = range(EARLY, q_ref.shape[1] // HD)
    attend_own(kv_heads, late, q_ref, load_ref, acc_ref, top_ref, bias_ref, vx_ref)


def partner_of(source, position):
    if source in ("even", "odd"):
        above = (lax.rem(lax.div(position, 2), 2) == 0) == (source == "even")
        return jnp.where(above, 2, -2), jnp.where(above, 3, 0), jnp.where(above, 0, 3)
    above = (lax.rem(position, 2) == 0) == (source == "near")
    return jnp.where(above, 1, -1), jnp.where(above, 2, 1), jnp.where(above, 1, 2)


def pick_of(source, where_ref, members_ref, ref):
    position = where_ref[0]
    offset, column, _ = partner_of(source, position)
    entry = members_ref[0, column]
    if ref.shape[0] == BLOCK + PAD:
        return entry, 0, ref[BLOCK : BLOCK + 1, :BLOCK]
    tok = ref.shape[0] - PAD
    blocks = tok // BLOCK
    first = pl.multiple_of(jnp.clip(entry - (position + offset) * blocks, 0, blocks - 1) * BLOCK, BLOCK)
    return entry, first, ref[tok : tok + 1, pl.ds(first, BLOCK)]


def far_kernel(kv_heads, where_ref, members_ref, q_ref, column_ref, acc0_ref, top0_ref, acc1_ref, top1_ref, *refs):
    source_refs = refs[: len(SOURCES)]
    out_ref, bias_ref, kx_ref, vx_ref, kl_ref, done_ref, sems = refs[len(SOURCES) :]
    tok = q_ref.shape[0]
    far = len(SOURCES) * BLOCK
    firsts = []
    for slot, (source, ref) in enumerate(zip(SOURCES, source_refs)):
        entry, first, level = pick_of(source, where_ref, members_ref, ref)
        firsts.append(first)
        kl_ref[0:1, slot * BLOCK : (slot + 1) * BLOCK] = jnp.where(entry >= 0, level.astype(jnp.float32), 1e9)
    bias_ref[...] = bias_of(column_ref[...], kl_ref[0:1, :])
    vx_ref[:, HD:] = jnp.ones((far, HD), jnp.bfloat16)

    def out_copy(g, r):
        spot = (pl.ds(r, ROWS), pl.ds(g * GROUP * HD, GROUP * HD))
        return pltpu.make_async_copy(done_ref.at[spot], out_ref.at[spot], sems.at[g, r // ROWS])

    for g in range(kv_heads):
        cols = pl.ds(g * HD, HD)
        vcols = pl.ds((g + kv_heads) * HD, HD)
        for slot, ref in enumerate(source_refs):
            picked = pl.ds(firsts[slot], BLOCK)
            kx_ref[slot * BLOCK : (slot + 1) * BLOCK, :] = ref[picked, cols]
            vx_ref[slot * BLOCK : (slot + 1) * BLOCK, :HD] = ref[picked, vcols]
        for r in range(0, tok, ROWS):
            rows = pl.ds(r, ROWS)
            for h in range(g * GROUP, (g + 1) * GROUP):
                head = pl.ds(h * HD, HD)
                if h < EARLY:
                    acc_ref, top_ref, spot = acc0_ref, top0_ref, pl.ds(h * HD, HD)
                else:
                    acc_ref, top_ref, spot = acc1_ref, top1_ref, pl.ds((h - EARLY) * HD, HD)
                old = top_ref[rows, spot]
                s = lax.dot_general(q_ref[rows, head], kx_ref[...], NT, preferred_element_type=jnp.float32)
                s = s * SCALE + bias_ref[rows, :]
                tops = [s[:, i : i + HD] for i in range(0, far, HD)]
                top = jnp.max(functools.reduce(jnp.maximum, tops, old), axis=1, keepdims=True)
                p = jnp.exp2(s - top).astype(jnp.bfloat16)
                o = lax.dot_general(p, vx_ref[...], NN, preferred_element_type=jnp.float32)
                share = jnp.exp2(old - top)
                mixed = (o[:, :HD] + share * acc_ref[rows, spot]) / (o[:, HD:] + share)
                done_ref[rows, head] = mixed.astype(jnp.bfloat16)
            out_copy(g, r).start()
    for g in range(kv_heads):
        for r in range(0, tok, ROWS):
            out_copy(g, r).wait()


def pairs_of(size, kind):
    if kind == "near":
        edges = [(i, i + 1) for i in range(0, size - 1, 2)]
        return [p for a, b in edges for p in ((a, b), (b, a))]
    if kind == "diag":
        edges = [(i, i + 1) for i in range(1, size - 1, 2)]
        return [p for a, b in edges for p in ((a, b), (b, a))]
    edges = [(i, i + 2) for i in range(size - 2) if (i // 2) % 2 == (kind == "odd")]
    return [p for a, b in edges for p in ((a, b), (b, a))]


def cost_of(tok, keys, heads):
    return pl.CostEstimate(
        flops=4 * tok * keys * heads * HD, transcendentals=tok * keys * heads, bytes_accessed=8 << 20
    )


def local(queries, keys, values, levels, members):
    tok = queries.shape[0]
    kv_heads = keys.shape[1] // HD
    heads = queries.shape[1] // HD
    size = lax.axis_size("seq")
    where = lax.axis_index("seq").astype(jnp.int32)[None]
    level_line = levels[None, :]
    send = lambda array, kind: lax.ppermute(array, "seq", pairs_of(size, kind))
    width = 2 * keys.shape[1]

    asked = {kind: send(members, kind) for kind in PICKED}
    wide = lambda count: jax.ShapeDtypeStruct((tok, count * HD), jnp.float32)
    rows_type = jax.ShapeDtypeStruct((tok, heads * HD), jnp.bfloat16)
    stay = lambda array: pltpu.with_memory_space_constraint(array, pltpu.HBM)
    own_scratch = [pltpu.VMEM((tok, tok), jnp.float32), pltpu.VMEM((tok, 2 * HD), jnp.bfloat16)]
    load, rows_in, column, acc0, top0 = pl.pallas_call(
        functools.partial(pack_kernel, kv_heads),
        in_specs=[HBM] * 4,
        out_specs=[VMEM] * 5,
        out_shape=[
            jax.ShapeDtypeStruct((tok + PAD, width), jnp.bfloat16),
            rows_type,
            wide(1),
            wide(EARLY),
            wide(EARLY),
        ],
        scratch_shapes=[pltpu.VMEM((1, tok), jnp.int32)] + own_scratch + [pltpu.SemaphoreType.DMA((5,))],
        compiler_params=PARAMS,
        cost_estimate=cost_of(tok, tok, EARLY),
    )(stay(keys), stay(values), stay(queries), stay(level_line))
    load, asked = lax.optimization_barrier((load, asked))
    arrived = {kind: send(load, kind) for kind in SOURCES if kind not in PICKED}
    pieces = pl.pallas_call(
        functools.partial(piece_kernel, PICKED),
        in_specs=[SMEM] * (1 + len(PICKED)) + [VMEM],
        out_specs=[VMEM] * len(PICKED),
        out_shape=[jax.ShapeDtypeStruct((BLOCK + PAD, width), jnp.bfloat16)] * len(PICKED),
        compiler_params=PARAMS,
        cost_estimate=pl.CostEstimate(flops=0, transcendentals=0, bytes_accessed=8 << 20),
    )(where, *[asked[kind] for kind in PICKED], load)
    arrived |= {kind: send(piece, kind) for kind, piece in zip(PICKED, pieces)}

    acc1, top1 = pl.pallas_call(
        functools.partial(own_kernel, kv_heads),
        in_specs=[VMEM] * 3,
        out_specs=[VMEM] * 2,
        out_shape=[wide(heads - EARLY)] * 2,
        scratch_shapes=own_scratch,
        compiler_params=PARAMS,
        cost_estimate=cost_of(tok, tok, heads - EARLY),
    )(rows_in, load, column)

    far = len(SOURCES) * BLOCK
    return pl.pallas_call(
        functools.partial(far_kernel, kv_heads),
        in_specs=[SMEM] * 2 + [VMEM] * (6 + len(SOURCES)),
        out_specs=HBM,
        out_shape=rows_type,
        scratch_shapes=[
            pltpu.VMEM((tok, far), jnp.float32),
            pltpu.VMEM((far, HD), jnp.bfloat16),
            pltpu.VMEM((far, 2 * HD), jnp.bfloat16),
            pltpu.VMEM((8, far), jnp.float32),
            pltpu.VMEM((tok, heads * HD), jnp.bfloat16),
            pltpu.SemaphoreType.DMA((kv_heads, tok // ROWS)),
        ],
        compiler_params=PARAMS,
        cost_estimate=cost_of(tok, far, heads),
    )(where, members, rows_in, column, acc0, top0, acc1, top1, *[arrived[kind] for kind in SOURCES])


def solution(mesh):
    placed = (
        P(("grp", "seq"), "head"),
        P(("grp", "seq"), "head"),
        P(("grp", "seq"), "head"),
        P(("grp", "seq")),
        P(("grp", "seq"), None),
    )
    return jax.shard_map(
        local, mesh=mesh, in_specs=placed, out_specs=P(("grp", "seq"), "head"), check_vma=False
    )
```

time: 44.7 us -> 32.9 us (0.74)
  the two profiles are of different devices: /device:TPU:28 before, /device:TPU:10 now
where the time goes in v4:
time: 32.9 us; the launch traced here: 32.5 us
  starting transfers between devices  16.3 us (50%)
  Pallas kernels  15.1 us (46%)
  waiting for transfers between devices  0.95 us (3%)
    ppermute x8, starting transfers between devices, local(): send = lambda array, kind: lax.ppermute(array, 'seq', pairs_of(size, kind))  16.3 us
    pallas_call x1, Pallas kernels, local(): pl.pallas_call(functools.partial(far_kernel, kv_heads), in_specs=[SMEM] *...  7.26 us
    pallas_call x1, Pallas kernels, local(): pl.pallas_call(functools.partial(own_kernel, kv_heads), in_specs=[VMEM] *...  5.01 us
    pallas_call x1, Pallas kernels, local(): pl.pallas_call(functools.partial(pack_kernel, kv_heads), in_specs=[HBM] *...  2.22 us
    ppermute x8, waiting for transfers between devices, local(): send = lambda array, kind: lax.ppermute(array, 'seq', pairs_of(size, kind))  0.95 us
  transfers between devices with their start and end apart: 8, of which 1 were waited for; matrix products, arithmetic and copies ran while one was open for 0% of the time, Pallas kernels for 22%

profile of v4, /device:TPU:10, one launch (start us, length us, event | category | flops | bytes accessed | tf_op | source)
XLA Modules:
  0.0 32.5 jit_solution(12114768381842299592)
XLA Ops:
  0.0 0.5 %collective-permute-start.2 = (s32[1,4]{1,0:T(1,128)}, s32[1,4]{1,0:T(1,128)S(1)}, u32[]{:S(2)}, u32[]{:S(2)}) collective-permute-start(s32[1,4]{1,0:T(1,128)} %members_ref.1), channel_id=1, source_target_pairs={{0,2},{2,0},{4,6},{6,4},{8,10},{10,8},{12,14},{14,12},{1,3},{3,1},... | collective-permute-start | bytes 56 | tf_op jit(solution)/shard_map/ppermute | solution.py:202
  0.5 0.0 collective-permute-start.1
  0.5 6.0 %collective-permute-start = (s32[1,4]{1,0:T(1,128)}, s32[1,4]{1,0:T(1,128)S(1)}, u32[]{:S(2)}, u32[]{:S(2)}) collective-permute-start(s32[1,4]{1,0:T(1,128)} %members_ref.1), channel_id=1, source_target_pairs={{2,4},{4,2},{6,8},{8,6},{10,12},{12,10},{3,5},{5,3},{7,9},{9,7},{1... | collective-permute-start | bytes 56 | tf_op jit(solution)/shard_map/ppermute | solution.py:202
  6.5 2.4 %collective-permute-start.3 = (s32[1,4]{1,0:T(1,128)}, s32[1,4]{1,0:T(1,128)S(1)}, u32[]{:S(2)}, u32[]{:S(2)}) collective-permute-start(s32[1,4]{1,0:T(1,128)} %members_ref.1), channel_id=1, source_target_pairs={{4,8},{8,4},{6,10},{10,6},{5,9},{9,5},{7,11},{11,7},{20,24},{24,20... | collective-permute-start | bytes 56 | tf_op jit(solution)/shard_map/ppermute | solution.py:202
  8.9 2.2 %shard_map.55 = (bf16[528,512]{1,0:T(8,128)(2,1)S(1)}, bf16[512,2048]{1,0:T(8,128)(2,1)S(1)}, f32[512,128]{1,0:T(8,128)S(1)}, f32[512,256]{1,0:T(8,128)S(1)}, f32[512,256]{1,0:T(8,128)S(1)}) custom-call(bf16[512,256]{1,0:T(8,128)(2,1)} %k_hbm.1, bf16[512,256]{1,0:T(8,128)(2,1)} %v_hbm.1, bf16[512,2048]{1,0:T(8,128)(2,1)} %q_hbm.1, s32[1,512]{1,0:T(1,128)} %bitcast.2), custom_call_target="tpu_custom_call" | custom-call | flops 268435456 | bytes 8388608 | tf_op jit(solution)/shard_map/pallas_call | solution.py:210
  11.1 0.0 collective-permute-done.2.refs_2_
  11.1 0.0 collective-permute-done.1.refs_0_
  11.1 0.0 collective-permute-done.refs_3_
  11.2 0.9 %collective-permute-done.3.refs_1_ = s32[1,4]{1,0:T(1,128)S(1)} collective-permute-done((s32[1,4]{1,0:T(1,128)}, s32[1,4]{1,0:T(1,128)S(1)}, u32[]{:S(2)}, u32[]{:S(2)}) %collective-permute-start.3) | collective-permute-done | bytes 48 | tf_op jit(solution)/shard_map/ppermute | solution.py:202
  12.1 0.6 %shard_map.57 = (bf16[144,512]{1,0:T(8,128)(2,1)S(1)}, bf16[144,512]{1,0:T(8,128)(2,1)S(1)}, bf16[144,512]{1,0:T(8,128)(2,1)S(1)}, bf16[144,512]{1,0:T(8,128)(2,1)S(1)}) custom-call(s32[1]{0:T(128)} %bitcast.where_ref, s32[1,4]{1,0:T(1,128)S(1)} %collective-permute-done.1.refs_0_, s32[1,4]{1,0:T(1,128)S(1)} %collective-permute-done.3.refs_1_, ...), custom_call_target="tpu_custom_call" | custom-call | bytes 8388608 | tf_op jit(solution)/shard_map/pallas_call | solution.py:227
  12.7 0.1 collective-permute-start.4
  12.8 0.1 collective-permute-start.5
  12.9 2.6 %collective-permute-start.6 = (bf16[144,512]{1,0:T(8,128)(2,1)S(1)}, bf16[144,512]{1,0:T(8,128)(2,1)S(1)}, u32[]{:S(2)}, u32[]{:S(2)}) collective-permute-start(bf16[144,512]{1,0:T(8,128)(2,1)S(1)} %get-tuple-element.35), channel_id=1, source_target_pairs={{4,8},{8,4},{6,10},{10,6},{5,9},{9,5},{7,11},{11,7},{20,24},{24,20... | collective-permute-start | bytes 442376 | tf_op jit(solution)/shard_map/ppermute | solution.py:202
  15.4 4.7 %collective-permute-start.7 = (bf16[144,512]{1,0:T(8,128)(2,1)S(1)}, bf16[144,512]{1,0:T(8,128)(2,1)S(1)}, u32[]{:S(2)}, u32[]{:S(2)}) collective-permute-start(bf16[144,512]{1,0:T(8,128)(2,1)S(1)} %get-tuple-element.36), channel_id=1, source_target_pairs={{2,4},{4,2},{6,8},{8,6},{10,12},{12,10},{3,5},{5,3},{7,9},{9,7},{1... | collective-permute-start | bytes 442376 | tf_op jit(solution)/shard_map/ppermute | solution.py:202
  20.2 0.0 copy-start
  20.2 5.0 %shard_map.56 = (f32[512,1792]{1,0:T(8,128)S(1)}, f32[512,1792]{1,0:T(8,128)S(1)}) custom-call(bf16[512,2048]{1,0:T(8,128)(2,1)S(1)} %get-tuple-element.21.q_ref, bf16[528,512]{1,0:T(8,128)(2,1)S(1)} %get-tuple-element.26.load_ref.refs_4_, f32[512,128]{1,0:T(8,128)S(1)} %get-tuple-element.22.column_ref), custom_call_target="tpu_custom_call" | custom-call | flops 1879048192 | bytes 8388608 | tf_op jit(solution)/shard_map/pallas_call | solution.py:237
  25.2 0.0 collective-permute-done.4.refs_0_
  25.2 0.0 collective-permute-done.5.refs_1_
  25.2 0.0 collective-permute-done.6.refs_2_
  25.2 0.0 collective-permute-done.7.refs_3_
  25.2 0.0 copy-done
  25.3 7.3 %shard_map.58 = bf16[512,2048]{1,0:T(8,128)(2,1)} custom-call(s32[1]{0:T(128)} %bitcast.where_ref, s32[1,4]{1,0:T(1,128)S(1)} %copy-done, bf16[512,2048]{1,0:T(8,128)(2,1)S(1)} %get-tuple-element.21.q_ref, f32[512,128]{1,0:T(8,128)S(1)} %get-tuple-element.22.column_ref, f32[512,256]{1,0:T(8,128)S(1)} %get-tuple-element.23.acc0_ref, ...), custom_call_target="tpu_custom_call" | custom-call | flops 2147483648 | bytes 8388608 | tf_op jit(solution)/shard_map/pallas_call | solution.py:248
Async XLA Ops:
  0.0 11.1 %collective-permute-start.2 = (s32[1,4]{1,0:T(1,128)}, s32[1,4]{1,0:T(1,128)S(1)}, u32[]{:S(2)}, u32[]{:S(2)}) collective-permute-start(s32[1,4]{1,0:T(1,128)} %members_ref.1), channel_id=1, source_target_pairs={{0,2},{2,0},{4,6},{6,4},{8,10},{10,8},{12,14},{14,12},{1,3},{3,1},... | collective-permute-start | bytes 56 | tf_op jit(solution)/shard_map/ppermute | solution.py:202
  0.5 10.6 %collective-permute-start.1 = (s32[1,4]{1,0:T(1,128)}, s32[1,4]{1,0:T(1,128)S(1)}, u32[]{:S(2)}, u32[]{:S(2)}) collective-permute-start(s32[1,4]{1,0:T(1,128)} %members_ref.1), channel_id=1, source_target_pairs={{0,4},{4,0},{2,6},{6,2},{8,12},{12,8},{10,14},{14,10},{1,5},{5,1},... | collective-permute-start | bytes 56 | tf_op jit(solution)/shard_map/ppermute | solution.py:202
  0.5 10.6 %collective-permute-start = (s32[1,4]{1,0:T(1,128)}, s32[1,4]{1,0:T(1,128)S(1)}, u32[]{:S(2)}, u32[]{:S(2)}) collective-permute-start(s32[1,4]{1,0:T(1,128)} %members_ref.1), channel_id=1, source_target_pairs={{2,4},{4,2},{6,8},{8,6},{10,12},{12,10},{3,5},{5,3},{7,9},{9,7},{1... | collective-permute-start | bytes 56 | tf_op jit(solution)/shard_map/ppermute | solution.py:202
  6.5 5.6 %collective-permute-start.3 = (s32[1,4]{1,0:T(1,128)}, s32[1,4]{1,0:T(1,128)S(1)}, u32[]{:S(2)}, u32[]{:S(2)}) collective-permute-start(s32[1,4]{1,0:T(1,128)} %members_ref.1), channel_id=1, source_target_pairs={{4,8},{8,4},{6,10},{10,6},{5,9},{9,5},{7,11},{11,7},{20,24},{24,20... | collective-permute-start | bytes 56 | tf_op jit(solution)/shard_map/ppermute | solution.py:202
  12.7 12.5 %collective-permute-start.4 = (bf16[144,512]{1,0:T(8,128)(2,1)S(1)}, bf16[144,512]{1,0:T(8,128)(2,1)S(1)}, u32[]{:S(2)}, u32[]{:S(2)}) collective-permute-start(bf16[144,512]{1,0:T(8,128)(2,1)S(1)} %get-tuple-element.33), channel_id=1, source_target_pairs={{0,4},{4,0},{2,6},{6,2},{8,12},{12,8},{10,14},{14,10},{1,5},{5,1},... | collective-permute-start | bytes 442376 | tf_op jit(solution)/shard_map/ppermute | solution.py:202
  12.8 12.4 %collective-permute-start.5 = (bf16[144,512]{1,0:T(8,128)(2,1)S(1)}, bf16[144,512]{1,0:T(8,128)(2,1)S(1)}, u32[]{:S(2)}, u32[]{:S(2)}) collective-permute-start(bf16[144,512]{1,0:T(8,128)(2,1)S(1)} %get-tuple-element.34), channel_id=1, source_target_pairs={{0,2},{2,0},{4,6},{6,4},{8,10},{10,8},{12,14},{14,12},{1,3},{3,1},... | collective-permute-start | bytes 442376 | tf_op jit(solution)/shard_map/ppermute | solution.py:202
  12.9 12.4 %collective-permute-start.6 = (bf16[144,512]{1,0:T(8,128)(2,1)S(1)}, bf16[144,512]{1,0:T(8,128)(2,1)S(1)}, u32[]{:S(2)}, u32[]{:S(2)}) collective-permute-start(bf16[144,512]{1,0:T(8,128)(2,1)S(1)} %get-tuple-element.35), channel_id=1, source_target_pairs={{4,8},{8,4},{6,10},{10,6},{5,9},{9,5},{7,11},{11,7},{20,24},{24,20... | collective-permute-start | bytes 442376 | tf_op jit(solution)/shard_map/ppermute | solution.py:202
  15.4 9.8 %collective-permute-start.7 = (bf16[144,512]{1,0:T(8,128)(2,1)S(1)}, bf16[144,512]{1,0:T(8,128)(2,1)S(1)}, u32[]{:S(2)}, u32[]{:S(2)}) collective-permute-start(bf16[144,512]{1,0:T(8,128)(2,1)S(1)} %get-tuple-element.36), channel_id=1, source_target_pairs={{2,4},{4,2},{6,8},{8,6},{10,12},{12,10},{3,5},{5,3},{7,9},{9,7},{1... | collective-permute-start | bytes 442376 | tf_op jit(solution)/shard_map/ppermute | solution.py:202
  20.2 5.1 %copy-start = (s32[1,4]{1,0:T(1,128)S(1)}, s32[1,4]{1,0:T(1,128)}, u32[]{:S(2)}) copy-start(s32[1,4]{1,0:T(1,128)} %members_ref.1) | copy-start | bytes 52

commit v5 on v4

--- a/solution.py
+++ b/solution.py
@@ -13,8 +13,9 @@
 ROWS = 256
 PAD = 16
 EARLY = 2
+SPAN = 4
 PICKED = ("even", "odd", "near", "diag")
-SOURCES = ("even", "near", "odd", "diag")
+SOURCES = ("near", "even", "odd", "diag")
 SCALE = HD ** (-0.5) * 1.4426950408889634
 HIDDEN = -1e30
 NT = (((1,), (1,)), ((), ()))
@@ -140,9 +141,9 @@
     bias_ref[...] = bias_of(column_ref[...], kl_ref[0:1, :])
     vx_ref[:, HD:] = jnp.ones((far, HD), jnp.bfloat16)
 
-    def out_copy(g, r):
-        spot = (pl.ds(r, ROWS), pl.ds(g * GROUP * HD, GROUP * HD))
-        return pltpu.make_async_copy(done_ref.at[spot], out_ref.at[spot], sems.at[g, r // ROWS])
+    def out_copy(h, r):
+        spot = (pl.ds(r, ROWS), pl.ds(h * HD, SPAN * HD))
+        return pltpu.make_async_copy(done_ref.at[spot], out_ref.at[spot], sems.at[h // SPAN, r // ROWS])
 
     for g in range(kv_heads):
         cols = pl.ds(g * HD, HD)
@@ -169,10 +170,11 @@
                 share = jnp.exp2(old - top)
                 mixed = (o[:, :HD] + share * acc_ref[rows, spot]) / (o[:, HD:] + share)
                 done_ref[rows, head] = mixed.astype(jnp.bfloat16)
-            out_copy(g, r).start()
-    for g in range(kv_heads):
+                if h % SPAN == SPAN - 1:
+                    out_copy(h - SPAN + 1, r).start()
+    for h in range(0, kv_heads * GROUP, SPAN):
         for r in range(0, tok, ROWS):
-            out_copy(g, r).wait()
+            out_copy(h, r).wait()
 
 
 def pairs_of(size, kind):
@@ -256,7 +258,7 @@
             pltpu.VMEM((far, 2 * HD), jnp.bfloat16),
             pltpu.VMEM((8, far), jnp.float32),
             pltpu.VMEM((tok, heads * HD), jnp.bfloat16),
-            pltpu.SemaphoreType.DMA((kv_heads, tok // ROWS)),
+            pltpu.SemaphoreType.DMA((heads // SPAN, tok // ROWS)),
         ],
         compiler_params=PARAMS,
         cost_estimate=cost_of(tok, far, heads),

time: 32.9 us -> 32.8 us (level)
  no operation moved by 1% of the time
where the time goes in v5:
time: 32.8 us; the launch traced here: 32.4 us
  starting transfers between devices  16.2 us (49%)
  Pallas kernels  15.1 us (46%)
  waiting for transfers between devices  0.95 us (3%)
    ppermute x8, starting transfers between devices, local(): send = lambda array, kind: lax.ppermute(array, 'seq', pairs_of(size, kind))  16.2 us
    pallas_call x1, Pallas kernels, local(): pl.pallas_call(functools.partial(far_kernel, kv_heads), in_specs=[SMEM] *...  7.22 us
    pallas_call x1, Pallas kernels, local(): pl.pallas_call(functools.partial(own_kernel, kv_heads), in_specs=[VMEM] *...  5.01 us
    pallas_call x1, Pallas kernels, local(): pl.pallas_call(functools.partial(pack_kernel, kv_heads), in_specs=[HBM] *...  2.22 us
    ppermute x8, waiting for transfers between devices, local(): send = lambda array, kind: lax.ppermute(array, 'seq', pairs_of(size, kind))  0.95 us
  transfers between devices with their start and end apart: 8, of which 1 were waited for; matrix products, arithmetic and copies ran while one was open for 0% of the time, Pallas kernels for 22%

profile of v5, /device:TPU:10, one launch (start us, length us, event | category | flops | bytes accessed | tf_op | source)
XLA Modules:
  0.0 32.4 jit_solution(13935441504944746425)
XLA Ops:
  0.0 0.5 %collective-permute-start.2 = (s32[1,4]{1,0:T(1,128)}, s32[1,4]{1,0:T(1,128)S(1)}, u32[]{:S(2)}, u32[]{:S(2)}) collective-permute-start(s32[1,4]{1,0:T(1,128)} %members_ref.1), channel_id=1, source_target_pairs={{0,2},{2,0},{4,6},{6,4},{8,10},{10,8},{12,14},{14,12},{1,3},{3,1},... | collective-permute-start | bytes 56 | tf_op jit(solution)/shard_map/ppermute | solution.py:204
  0.5 0.0 collective-permute-start.1
  0.5 6.0 %collective-permute-start = (s32[1,4]{1,0:T(1,128)}, s32[1,4]{1,0:T(1,128)S(1)}, u32[]{:S(2)}, u32[]{:S(2)}) collective-permute-start(s32[1,4]{1,0:T(1,128)} %members_ref.1), channel_id=1, source_target_pairs={{2,4},{4,2},{6,8},{8,6},{10,12},{12,10},{3,5},{5,3},{7,9},{9,7},{1... | collective-permute-start | bytes 56 | tf_op jit(solution)/shard_map/ppermute | solution.py:204
  6.5 2.4 %collective-permute-start.3 = (s32[1,4]{1,0:T(1,128)}, s32[1,4]{1,0:T(1,128)S(1)}, u32[]{:S(2)}, u32[]{:S(2)}) collective-permute-start(s32[1,4]{1,0:T(1,128)} %members_ref.1), channel_id=1, source_target_pairs={{4,8},{8,4},{6,10},{10,6},{5,9},{9,5},{7,11},{11,7},{20,24},{24,20... | collective-permute-start | bytes 56 | tf_op jit(solution)/shard_map/ppermute | solution.py:204
  8.9 2.2 %shard_map.55 = (bf16[528,512]{1,0:T(8,128)(2,1)S(1)}, bf16[512,2048]{1,0:T(8,128)(2,1)S(1)}, f32[512,128]{1,0:T(8,128)S(1)}, f32[512,256]{1,0:T(8,128)S(1)}, f32[512,256]{1,0:T(8,128)S(1)}) custom-call(bf16[512,256]{1,0:T(8,128)(2,1)} %k_hbm.1, bf16[512,256]{1,0:T(8,128)(2,1)} %v_hbm.1, bf16[512,2048]{1,0:T(8,128)(2,1)} %q_hbm.1, s32[1,512]{1,0:T(1,128)} %bitcast.2), custom_call_target="tpu_custom_call" | custom-call | flops 268435456 | bytes 8388608 | tf_op jit(solution)/shard_map/pallas_call | solution.py:212
  11.1 0.0 collective-permute-done.2.refs_2_
  11.1 0.0 collective-permute-done.1.refs_0_
  11.1 0.0 collective-permute-done.refs_3_
  11.2 0.9 %collective-permute-done.3.refs_1_ = s32[1,4]{1,0:T(1,128)S(1)} collective-permute-done((s32[1,4]{1,0:T(1,128)}, s32[1,4]{1,0:T(1,128)S(1)}, u32[]{:S(2)}, u32[]{:S(2)}) %collective-permute-start.3) | collective-permute-done | bytes 48 | tf_op jit(solution)/shard_map/ppermute | solution.py:204
  12.1 0.6 %shard_map.57 = (bf16[144,512]{1,0:T(8,128)(2,1)S(1)}, bf16[144,512]{1,0:T(8,128)(2,1)S(1)}, bf16[144,512]{1,0:T(8,128)(2,1)S(1)}, bf16[144,512]{1,0:T(8,128)(2,1)S(1)}) custom-call(s32[1]{0:T(128)} %bitcast.where_ref, s32[1,4]{1,0:T(1,128)S(1)} %collective-permute-done.1.refs_0_, s32[1,4]{1,0:T(1,128)S(1)} %collective-permute-done.3.refs_1_, ...), custom_call_target="tpu_custom_call" | custom-call | bytes 8388608 | tf_op jit(solution)/shard_map/pallas_call | solution.py:229
  12.7 0.1 collective-permute-start.4
  12.8 0.1 collective-permute-start.5
  12.9 2.6 %collective-permute-start.6 = (bf16[144,512]{1,0:T(8,128)(2,1)S(1)}, bf16[144,512]{1,0:T(8,128)(2,1)S(1)}, u32[]{:S(2)}, u32[]{:S(2)}) collective-permute-start(bf16[144,512]{1,0:T(8,128)(2,1)S(1)} %get-tuple-element.35), channel_id=1, source_target_pairs={{4,8},{8,4},{6,10},{10,6},{5,9},{9,5},{7,11},{11,7},{20,24},{24,20... | collective-permute-start | bytes 442376 | tf_op jit(solution)/shard_map/ppermute | solution.py:204
  15.4 4.6 %collective-permute-start.7 = (bf16[144,512]{1,0:T(8,128)(2,1)S(1)}, bf16[144,512]{1,0:T(8,128)(2,1)S(1)}, u32[]{:S(2)}, u32[]{:S(2)}) collective-permute-start(bf16[144,512]{1,0:T(8,128)(2,1)S(1)} %get-tuple-element.36), channel_id=1, source_target_pairs={{2,4},{4,2},{6,8},{8,6},{10,12},{12,10},{3,5},{5,3},{7,9},{9,7},{1... | collective-permute-start | bytes 442376 | tf_op jit(solution)/shard_map/ppermute | solution.py:204
  20.1 0.0 copy-start
  20.1 5.0 %shard_map.56 = (f32[512,1792]{1,0:T(8,128)S(1)}, f32[512,1792]{1,0:T(8,128)S(1)}) custom-call(bf16[512,2048]{1,0:T(8,128)(2,1)S(1)} %get-tuple-element.21.q_ref, bf16[528,512]{1,0:T(8,128)(2,1)S(1)} %get-tuple-element.26.load_ref.refs_4_, f32[512,128]{1,0:T(8,128)S(1)} %get-tuple-element.22.column_ref), custom_call_target="tpu_custom_call" | custom-call | flops 1879048192 | bytes 8388608 | tf_op jit(solution)/shard_map/pallas_call | solution.py:239
  25.1 0.0 collective-permute-done.4.refs_0_
  25.1 0.0 collective-permute-done.5.refs_1_
  25.1 0.0 collective-permute-done.6.refs_2_
  25.2 0.0 collective-permute-done.7.refs_3_
  25.2 0.0 copy-done
  25.2 7.2 %shard_map.58 = bf16[512,2048]{1,0:T(8,128)(2,1)} custom-call(s32[1]{0:T(128)} %bitcast.where_ref, s32[1,4]{1,0:T(1,128)S(1)} %copy-done, bf16[512,2048]{1,0:T(8,128)(2,1)S(1)} %get-tuple-element.21.q_ref, f32[512,128]{1,0:T(8,128)S(1)} %get-tuple-element.22.column_ref, f32[512,256]{1,0:T(8,128)S(1)} %get-tuple-element.23.acc0_ref, ...), custom_call_target="tpu_custom_call" | custom-call | flops 2147483648 | bytes 8388608 | tf_op jit(solution)/shard_map/pallas_call | solution.py:250
Async XLA Ops:
  0.0 11.1 %collective-permute-start.2 = (s32[1,4]{1,0:T(1,128)}, s32[1,4]{1,0:T(1,128)S(1)}, u32[]{:S(2)}, u32[]{:S(2)}) collective-permute-start(s32[1,4]{1,0:T(1,128)} %members_ref.1), channel_id=1, source_target_pairs={{0,2},{2,0},{4,6},{6,4},{8,10},{10,8},{12,14},{14,12},{1,3},{3,1},... | collective-permute-start | bytes 56 | tf_op jit(solution)/shard_map/ppermute | solution.py:204
  0.5 10.6 %collective-permute-start.1 = (s32[1,4]{1,0:T(1,128)}, s32[1,4]{1,0:T(1,128)S(1)}, u32[]{:S(2)}, u32[]{:S(2)}) collective-permute-start(s32[1,4]{1,0:T(1,128)} %members_ref.1), channel_id=1, source_target_pairs={{0,4},{4,0},{2,6},{6,2},{8,12},{12,8},{10,14},{14,10},{1,5},{5,1},... | collective-permute-start | bytes 56 | tf_op jit(solution)/shard_map/ppermute | solution.py:204
  0.5 10.6 %collective-permute-start = (s32[1,4]{1,0:T(1,128)}, s32[1,4]{1,0:T(1,128)S(1)}, u32[]{:S(2)}, u32[]{:S(2)}) collective-permute-start(s32[1,4]{1,0:T(1,128)} %members_ref.1), channel_id=1, source_target_pairs={{2,4},{4,2},{6,8},{8,6},{10,12},{12,10},{3,5},{5,3},{7,9},{9,7},{1... | collective-permute-start | bytes 56 | tf_op jit(solution)/shard_map/ppermute | solution.py:204
  6.5 5.6 %collective-permute-start.3 = (s32[1,4]{1,0:T(1,128)}, s32[1,4]{1,0:T(1,128)S(1)}, u32[]{:S(2)}, u32[]{:S(2)}) collective-permute-start(s32[1,4]{1,0:T(1,128)} %members_ref.1), channel_id=1, source_target_pairs={{4,8},{8,4},{6,10},{10,6},{5,9},{9,5},{7,11},{11,7},{20,24},{24,20... | collective-permute-start | bytes 56 | tf_op jit(solution)/shard_map/ppermute | solution.py:204
  12.7 12.4 %collective-permute-start.4 = (bf16[144,512]{1,0:T(8,128)(2,1)S(1)}, bf16[144,512]{1,0:T(8,128)(2,1)S(1)}, u32[]{:S(2)}, u32[]{:S(2)}) collective-permute-start(bf16[144,512]{1,0:T(8,128)(2,1)S(1)} %get-tuple-element.33), channel_id=1, source_target_pairs={{0,2},{2,0},{4,6},{6,4},{8,10},{10,8},{12,14},{14,12},{1,3},{3,1},... | collective-permute-start | bytes 442376 | tf_op jit(solution)/shard_map/ppermute | solution.py:204
  12.8 12.3 %collective-permute-start.5 = (bf16[144,512]{1,0:T(8,128)(2,1)S(1)}, bf16[144,512]{1,0:T(8,128)(2,1)S(1)}, u32[]{:S(2)}, u32[]{:S(2)}) collective-permute-start(bf16[144,512]{1,0:T(8,128)(2,1)S(1)} %get-tuple-element.34), channel_id=1, source_target_pairs={{0,4},{4,0},{2,6},{6,2},{8,12},{12,8},{10,14},{14,10},{1,5},{5,1},... | collective-permute-start | bytes 442376 | tf_op jit(solution)/shard_map/ppermute | solution.py:204
  12.9 12.3 %collective-permute-start.6 = (bf16[144,512]{1,0:T(8,128)(2,1)S(1)}, bf16[144,512]{1,0:T(8,128)(2,1)S(1)}, u32[]{:S(2)}, u32[]{:S(2)}) collective-permute-start(bf16[144,512]{1,0:T(8,128)(2,1)S(1)} %get-tuple-element.35), channel_id=1, source_target_pairs={{4,8},{8,4},{6,10},{10,6},{5,9},{9,5},{7,11},{11,7},{20,24},{24,20... | collective-permute-start | bytes 442376 | tf_op jit(solution)/shard_map/ppermute | solution.py:204
  15.4 9.7 %collective-permute-start.7 = (bf16[144,512]{1,0:T(8,128)(2,1)S(1)}, bf16[144,512]{1,0:T(8,128)(2,1)S(1)}, u32[]{:S(2)}, u32[]{:S(2)}) collective-permute-start(bf16[144,512]{1,0:T(8,128)(2,1)S(1)} %get-tuple-element.36), channel_id=1, source_target_pairs={{2,4},{4,2},{6,8},{8,6},{10,12},{12,10},{3,5},{5,3},{7,9},{9,7},{1... | collective-permute-start | bytes 442376 | tf_op jit(solution)/shard_map/ppermute | solution.py:204
  20.1 5.1 %copy-start = (s32[1,4]{1,0:T(1,128)S(1)}, s32[1,4]{1,0:T(1,128)}, u32[]{:S(2)}) copy-start(s32[1,4]{1,0:T(1,128)} %members_ref.1) | copy-start | bytes 52
